TPU v7x, 512 devices: a whole 4x4x16 slice. The times are simulated.
512 devices in a mesh: gx: 32 (over z, core), gy: 16 (over x, y).
Axes of the slice: x: 4, y: 4, z: 16, core: 2. Of those that a mesh axis runs over, the one named last changes fastest.
Arguments:
- right_side: float32 [512, 512, 128], P('gx', 'gy'), may hold values from -1 to 2
- screening: float32 [512, 512, 128], P('gx', 'gy'), may hold values from 0.5 to 5
- active_blocks: int32 [32, 16, 12], P('gx', 'gy'), may hold values from -1 to 15, as said below
- visible_bricks: int32 [32, 16, 8], P('gx', 'gy'), may hold values from -1 to 15, as said below
Outputs:
- indicator: float32 [512, 512, 128], P('gx', 'gy')
- crossing: float32 [256, 16, 3, 4096], P('gx', 'gy')
Inputs may be any that keep to these rules, and one draw needn't show every extreme that they name: `active_blocks`: each device's row lists distinct block numbers of that device's 16 blocks first, then -1 in the unused slots; at least one entry is a block number; some device fills all 12 slots and some leaves slots unused. `visible_bricks`: each device's row lists distinct block numbers of that device's 16 blocks first, then -1 in the unused slots; at least one entry is a block number; some device fills all 8 slots.
All inputs are finite; a program needn't handle non-finite values.
Results may differ from a plain program's by a relative error of at most 0.0003.
Values sent between devices are 32-bit elements; how exact they have to be, the bound alone decides.
A program may use at most 64 MiB of HBM per device.

v0:
```python
import jax
import jax.numpy as jnp
from jax import lax
from jax.sharding import PartitionSpec as P

BLK = 16
ITERS = 3


MASS = (11.0 / 20.0, 13.0 / 60.0, 1.0 / 120.0)
STIFF = (1.0, -1.0 / 3.0, -1.0 / 6.0)
SHARP = 4.0


def with_halo(block, sides, width):
    for axis, dim in sides:
        count = lax.axis_size(axis)
        forward = [(i, i + 1) for i in range(count - 1)]
        backward = [(target, source) for source, target in forward]
        low = lax.ppermute(
            lax.slice_in_dim(block, block.shape[dim] - width, None, axis=dim), axis, forward
        )
        high = lax.ppermute(lax.slice_in_dim(block, 0, width, axis=dim), axis, backward)
        block = jnp.concatenate([low, block, high], axis=dim)
    return block


def from_behind(value, axis, steps):
    count = lax.axis_size(axis)
    first, last = (max(0, -steps), min(count, count - steps))
    return lax.ppermute(value, axis, [(source, source + steps) for source in range(first, last)])


def apply_axis(padded, axis, coef):
    count = padded.shape[axis] - 4

    def part(start):
        return lax.slice_in_dim(padded, start, start + count, axis=axis)

    return coef[0] * part(2) + coef[1] * (part(1) + part(3)) + coef[2] * (part(0) + part(4))


def pad_depth(field):
    return jnp.pad(field, ((0, 0), (0, 0), (2, 2)))


def operate(field, screening, mask):
    padded = with_halo(field, (("gx", 0), ("gy", 1)), 2)
    zpadded = pad_depth(padded)
    mass_z = apply_axis(zpadded, 2, MASS)
    stiff_z = apply_axis(zpadded, 2, STIFF)
    inner = apply_axis(stiff_z, 1, MASS) + apply_axis(mass_z, 1, STIFF)
    outer = apply_axis(mass_z, 1, MASS)
    return mask * (apply_axis(inner, 0, MASS) + apply_axis(outer, 0, STIFF) + screening * field)


def crossing_weight(low, high):
    lower = jax.nn.sigmoid(SHARP * low)
    upper = jax.nn.sigmoid(SHARP * high)
    return lower * (1.0 - upper) + (1.0 - lower) * upper


def squares(residual):
    return lax.psum(jnp.sum(residual * residual), ("gx", "gy"))


def body(right_side, screening, active_blocks, visible_bricks):
    cells_x, cells_y, cells_z = right_side.shape
    bx_dev, by_dev, bz_dev = (cells_x // BLK, cells_y // BLK, cells_z // BLK)
    entries = active_blocks.reshape(-1)
    numbers = jnp.arange(bx_dev * by_dev * bz_dev, dtype=jnp.int32)
    block_mask = jnp.any(numbers[:, None] == entries[None, :], axis=-1).astype(jnp.float32)
    block_mask = block_mask.reshape(bx_dev, 1, by_dev, 1, bz_dev, 1)
    mask = jnp.broadcast_to(block_mask, (bx_dev, BLK, by_dev, BLK, bz_dev, BLK)).reshape(
        right_side.shape
    )
    indicator = jnp.zeros_like(right_side)
    residual = mask * right_side
    direction = residual
    norm_now = squares(residual)
    for step in range(ITERS):
        image = operate(direction, screening, mask)
        alpha = norm_now / lax.psum(jnp.sum(direction * image), ("gx", "gy"))
        indicator = indicator + alpha * direction
        residual = residual - alpha * image
        if step + 1 < ITERS:
            norm_next = squares(residual)
            direction = residual + norm_next / norm_now * direction
            norm_now = norm_next
    local_count = jnp.sum((entries >= 0).astype(jnp.float32))
    total, count = lax.psum((jnp.sum(indicator), local_count), ("gx", "gy"))
    iso = total / (count * float(BLK**3))
    face_x = from_behind(indicator[:1], "gx", -1)
    face_y = from_behind(indicator[:, :1], "gy", -1)
    extended = jnp.concatenate((indicator, face_x), axis=0)
    face_y = jnp.pad(face_y, ((0, 1), (0, 0), (0, 0)))
    extended = jnp.concatenate((extended, face_y), axis=1)
    extended = jnp.pad(extended, ((0, 0), (0, 0), (0, 1)))

    def brick_weights(number):
        safe = jnp.maximum(number, 0)
        block_x = safe // (by_dev * bz_dev)
        block_y = safe // bz_dev % by_dev
        block_z = safe % bz_dev
        start = [block_x * BLK, block_y * BLK, block_z * BLK]
        region = lax.dynamic_slice(extended, start, (BLK + 1, BLK + 1, BLK + 1)) - iso
        base = region[:-1, :-1, :-1]
        result = jnp.stack(
            [
                crossing_weight(base, region[1:, :-1, :-1]),
                crossing_weight(base, region[:-1, 1:, :-1]),
                crossing_weight(base, region[:-1, :-1, 1:]),
            ]
        ).reshape(3, BLK * BLK * BLK)
        return jnp.where(number >= 0, result, jnp.zeros_like(result))

    bricks = visible_bricks.reshape(-1)
    weights = lax.map(brick_weights, bricks)
    crossing = weights.reshape(bricks.shape[0], 1, 3, BLK * BLK * BLK)
    return (indicator, crossing)


def solution(mesh):
    return jax.shard_map(
        body,
        mesh=mesh,
        in_specs=(
            P("gx", "gy", None),
            P("gx", "gy", None),
            P("gx", "gy", None),
            P("gx", "gy", None),
        ),
        out_specs=(P("gx", "gy", None), P("gx", "gy", None, None)),
        check_vma=False,
    )
```

profile of v0, /device:TPU:1, one launch (start us, length us, event | category | flops | bytes accessed | tf_op | source)
XLA Modules:
  0.0 715.7 jit_solution(11877553162940235299)
XLA Ops:
  1.7 4.9 collective-permute-start
  6.7 5.1 collective-permute-start.1
  12.7 2.4 collective-permute-start.2
  15.1 1.3 collective-permute-start.3
  16.5 3.2 collective-permute-done.3
  22.4 111.0 %all-reduce.6 = (f32[]{:T(128)}, f32[]{:T(128)}) all-reduce(f32[]{:T(128)} %get-tuple-element.101, f32[]{:T(128)} %get-tuple-element.100), channel_id=1, replica_groups=mesh['gx'=32,'gy'=16] {'gx','gy'}, use_global_device_ids=true, to_apply=%region_2.0 | all-reduce | flops 2 | bytes 16 | tf_op jit(solution)/shard_map/psum | solution.py:64
  135.4 98.7 %psum.58 = f32[]{:T(128)} all-reduce(f32[]{:T(128)} %get-tuple-element.120), channel_id=1, replica_groups=mesh['gx'=32,'gy'=16] {'gx','gy'}, use_global_device_ids=true, to_apply=%region_6.7 | all-reduce | flops 1 | bytes 8 | tf_op jit(solution)/shard_map/psum | solution.py:64
  235.5 4.2 collective-permute-start.4
  239.8 1.9 collective-permute-start.5
  241.7 3.3 collective-permute-done.5
  245.0 2.9 collective-permute-start.6
  247.9 1.3 collective-permute-start.7
  249.2 3.2 collective-permute-done.7
  254.6 102.6 %psum.59 = f32[]{:T(128)} all-reduce(f32[]{:T(128)} %get-tuple-element.118), channel_id=1, replica_groups=mesh['gx'=32,'gy'=16] {'gx','gy'}, use_global_device_ids=true, to_apply=%region_8.9 | all-reduce | flops 1 | bytes 8 | tf_op jit(solution)/shard_map/psum | solution.py:83
  359.2 99.5 %psum.60 = f32[]{:T(128)} all-reduce(f32[]{:T(128)} %multiply_reduce_fusion), channel_id=1, replica_groups=mesh['gx'=32,'gy'=16] {'gx','gy'}, use_global_device_ids=true, to_apply=%region_10.11 | all-reduce | flops 1 | bytes 8 | tf_op jit(solution)/shard_map/psum | solution.py:64
  460.1 4.2 collective-permute-start.8
  464.4 1.9 collective-permute-start.9
  466.3 3.3 collective-permute-done.9
  469.6 3.0 collective-permute-start.10
  473.9 3.2 collective-permute-done.11
  479.2 102.6 %psum.61 = f32[]{:T(128)} all-reduce(f32[]{:T(128)} %fusion.44), channel_id=1, replica_groups=mesh['gx'=32,'gy'=16] {'gx','gy'}, use_global_device_ids=true, to_apply=%region_12.13 | all-reduce | flops 1 | bytes 8 | tf_op jit(solution)/shard_map/psum | solution.py:83
  583.9 2.6 collective-permute-start.12
  588.5 101.4 %all-reduce.5 = (f32[]{:T(128)}, f32[]{:T(128)}) all-reduce(f32[]{:T(128)} %get-tuple-element.116, f32[]{:T(128)} %fusion.74), channel_id=1, replica_groups=mesh['gx'=32,'gy'=16] {'gx','gy'}, use_global_device_ids=true, to_apply=%region_14.15 | all-reduce | flops 2 | bytes 16 | tf_op jit(solution)/shard_map/psum | solution.py:91
  692.0 22.6 %while.13 = (s32[]{:T(128)}, f32[8,3,4096]{2,1,0:T(4,128)S(1)}, s32[8]{0:T(128)S(1)}, f32[17,33,129]{2,1,0:T(8,128)S(1)}, f32[]{:T(128)}, /*index=5*/s32[]{:T(12...) while((s32[]{:T(128)}, f32[8,3,4096]{2,1,0:T(4,128)S(1)}, ...), condition=%wide.region_18.19_spmd, body=%wide.region_17.18_spmd.sunk | while | flops 160596 | bytes 367507 | solution.py:118
  (113 shorter events, 27.1 us)
Async XLA Ops:
  0.6 0.7 copy-start.3
  0.6 1.0 copy-start
  1.7 10.1 %collective-permute-start = (f32[2,32,128]{2,1,0:T(8,128)S(1)}, f32[2,32,128]{2,1,0:T(8,128)S(1)}, u32[]{:S(2)}, u32[]{:S(2)}) collective-permute-start(f32[2,32,128]{2,1,0:T(8,128)S(1)} %get-tuple-element.148), channel_id=1, source_target_pairs={{0,16},{16,32},{32,48},{48,64},{64,80},{80,96},{96,112},{112,128},... | collective-permute-start | bytes 98312 | tf_op jit(solution)/shard_map/ppermute | solution.py:20
  6.7 6.0 collective-permute-start.1
  12.7 3.8 collective-permute-start.2
  15.1 4.5 collective-permute-start.3
  20.6 1.0 copy-start.1
  235.5 6.2 collective-permute-start.4
  239.8 5.2 collective-permute-start.5
  245.0 4.2 collective-permute-start.6
  247.9 4.5 collective-permute-start.7
  460.1 6.2 collective-permute-start.8
  464.4 5.2 collective-permute-start.9
  469.6 4.3 collective-permute-start.10
  472.6 4.5 collective-permute-start.11
  583.9 107.4 %copy-start.2 = (f32[16,32,128]{2,1,0:T(8,128)}, f32[16,32,128]{2,1,0:T(8,128)S(1)}, u32[]{:S(2)}) copy-start(f32[16,32,128]{2,1,0:T(8,128)S(1)} %get-tuple-element.117) | copy-start | bytes 786436
  583.9 107.3 %collective-permute-start.12 = (f32[1,32,128]{2,1,0:T(8,128)S(1)}, f32[1,32,128]{2,1,0:T(8,128)S(1)}, u32[]{:S(2)}, u32[]{:S(2)}) collective-permute-start(f32[1,32,128]{2,1,0:T(8,128)S(1)} %slice.475), channel_id=1, source_target_pairs={{16,0},{32,16},{48,32},{64,48},{80,64},{96,80},{112,96},{128,112},... | collective-permute-start | bytes 49160 | tf_op jit(solution)/shard_map/ppermute | solution.py:31
  586.5 104.7 %collective-permute-start.13 = (f32[16,1,128]{2,1,0:T(1,128)S(1)}, f32[16,1,128]{2,1,0:T(1,128)S(1)}, u32[]{:S(2)}, u32[]{:S(2)}) collective-permute-start(f32[16,1,128]{2,1,0:T(1,128)S(1)} %slice.476), channel_id=1, source_target_pairs={{1,0},{2,1},{3,2},{4,3},{5,4},{6,5},{7,6},{8,7},{9,8},{10,9},{11,1... | collective-permute-start | bytes 24584 | tf_op jit(solution)/shard_map/ppermute | solution.py:31
  691.3 0.7 copy-start.4
where the time goes:
time: 718 us; the launch traced here: 716 us
  blocking collectives  616 us (86%)
  starting transfers between devices  38.4 us (5%)
  waiting for transfers between devices  17.1 us (2%)
  other arithmetic  12.3 us (2%)
  loops' own time  11.8 us (2%)
  local copies, waits for them, and re-layouts  11.3 us (2%)
  between operations  9.04 us (1%)
    psum x3, blocking collectives, squares(): return lax.psum(jnp.sum(residual * residual), ('gx', 'gy'))  309 us
    psum x2, blocking collectives, body(): alpha = norm_now / lax.psum(jnp.sum(direction * image), ('gx', 'gy'))  205 us
    psum x1, blocking collectives, body(): total, count = lax.psum((jnp.sum(indicator), local_count), ('gx', 'gy'))  101 us
    ppermute x6, starting transfers between devices, with_halo(): lax.ppermute(lax.slice_in_dim(block, block.shape[dim] - width, None, axis...  21.7 us
    ppermute x6, waiting for transfers between devices, with_halo(): lax.ppermute(lax.slice_in_dim(block, 0, width, axis=dim), axis, backward)  17.1 us
  transfers between devices with their start and end apart: 14, of which 6 were waited for; matrix products, arithmetic and copies ran while one was open for 0% of the time, Pallas kernels for 0%

commit v1 on v0

v1 whole, which is shorter than its diff:
```python
import jax
import jax.numpy as jnp
from jax import lax
from jax.experimental import pallas as pl
from jax.experimental.pallas import tpu as pltpu
from jax.sharding import PartitionSpec as P

MESH = pl.DeviceIdType.MESH
BLK = 16
ACT = 12
VIS = 8
NGX = 32
NGY = 16
NZ = 16
SIGMA = 2.5
HR = 6
HS = 4
SCALE = 1.0 / 86400.0
NEIGHBOURS = [(1, 1), (1, -1), (-1, 1), (-1, -1), (0, 1), (0, -1), (1, 0), (-1, 0)]


def two_sum(a, b):
    s = a + b
    t = s - a
    return s, (a - (s - t)) + (b - t)


def quick_two_sum(a, b):
    s = a + b
    return s, b - (s - a)


def split(a):
    c = 4097.0 * a
    hi = c - (c - a)
    return hi, a - hi


def two_prod(a, b):
    p = a * b
    ah, al = split(a)
    bh, bl = split(b)
    return p, ((ah * bh - p) + ah * bl + al * bh) + al * bl


def dd_add(x, y):
    s, e = two_sum(x[0], y[0])
    return quick_two_sum(s, e + (x[1] + y[1]))


def dd_neg(x):
    return -x[0], -x[1]


def dd_sub(x, y):
    return dd_add(x, dd_neg(y))


def dd_mul(x, y):
    p, e = two_prod(x[0], y[0])
    return quick_two_sum(p, e + (x[0] * y[1] + x[1] * y[0]))


def dd_div(x, y):
    q = x[0] / y[0]
    r = dd_sub(x, dd_mul(y, (q, jnp.zeros_like(q))))
    return quick_two_sum(q, r[0] / y[0])


def cg_weights(mu):
    one = (jnp.ones_like(mu[0][0]), jnp.zeros_like(mu[0][0]))
    inv = dd_div(one, mu[0])
    row = [dd_mul(m, inv) for m in mu[1:]]
    a = row[0]
    level = [dd_sub(row[k + 1], dd_mul(a, row[k])) for k in range(4)]
    first = [(jnp.zeros_like(a[0]), jnp.zeros_like(a[0]))] + level
    central = []
    for _ in range(4):
        first = [dd_sub(first[k + 1], dd_mul(a, first[k])) for k in range(len(first) - 1)]
        central.append(first[0])
    m2, m3, m4, m5 = central
    tiny = 1e-30
    m2s = (jnp.maximum(m2[0], tiny), jnp.where(m2[0] > tiny, m2[1], 0.0))
    b1 = dd_div(m3, m2s)
    m22 = dd_mul(m2, m2)
    h2 = dd_sub(dd_sub(m4, dd_mul(b1, m3)), m22)
    h2s = jnp.maximum(h2[0], tiny)
    inner = dd_sub(dd_mul(b1, m3), dd_add(m4, m4))
    inner = dd_add(inner, dd_add(m22, m22))
    top = dd_add(m5, dd_mul(b1, inner))
    m23 = dd_mul(m2, m3)
    top = dd_sub(top, dd_add(m23, m23))
    d0 = a[0] + SIGMA
    d1 = jnp.clip(d0 + b1[0], 0.25, 9.0)
    d2 = jnp.clip(d0 + top[0] / h2s, 0.25, 9.0)
    beta1 = jnp.maximum(m2[0], 0.0)
    beta2 = jnp.clip(h2[0] / m2s[0], 0.0, 25.0)
    bb1 = d1 - d0
    minor = d1 * d2 - beta2
    y2 = 1.0 / (d0 * minor - beta1 * d2)
    y1 = -d2 * y2
    y0 = minor * y2
    c2 = y2
    c1 = y1 - y2 * (2.0 * a[0] + bb1)
    c0 = y0 - a[0] * y1 + y2 * (a[0] * a[0] + a[0] * bb1 - m2[0])
    return c0, c1, c2


def sigmoid4(v):
    return 1.0 / (1.0 + jnp.exp(-4.0 * v))


def crossing_weight(lower, upper):
    return lower * (1.0 - upper) + (1.0 - lower) * upper


def solve_kernel(rhs, scr, act, x_out, iso_out,
           R, S, M, U1, U2, MZ, SZ, IN, OUT, act_s, ar1, ar2, ar3, stage,
           lsem, ssem, rsem, asem, arsem):
    gx = lax.axis_index("gx")
    gy = lax.axis_index("gy")
    z = gx // 2
    core = lax.rem(gx, 2)

    def at_z(off, c):
        return lax.rem(z + off + NZ, NZ) * 2 + c

    bar = pltpu.get_barrier_semaphore()

    def tell(x, y):
        pl.semaphore_signal(bar, inc=1, device_id=(x, y), device_id_type=MESH)

    tell(at_z(-4, core), gy)
    for off in (4, -3, 3, -2, 2, -1, 1):
        for c in (0, 1):
            tell(at_z(off, c), gy)
    tell(at_z(0, 1 - core), gy)
    for j in range(1, NGY):
        tell(gx, lax.rem(gy + j, NGY))
    has = []
    for dx, dy in NEIGHBOURS:
        ok = None
        for cond in ([gx < NGX - 1] if dx == 1 else []) + ([gx > 0] if dx == -1 else []) + (
            [gy < NGY - 1] if dy == 1 else []) + ([gy > 0] if dy == -1 else []):
            ok = cond if ok is None else jnp.logical_and(ok, cond)
        has.append(ok)
    for dx, dy in NEIGHBOURS:
        if dx and dy:
            tell(lax.rem(gx + dx + NGX, NGX), lax.rem(gy + dy + NGY, NGY))

    loads = [
        pltpu.make_async_copy(act.at[0], act_s, lsem.at[0]),
        pltpu.make_async_copy(rhs, R.at[pl.ds(HR, 16), pl.ds(8, 32)], lsem.at[1]),
        pltpu.make_async_copy(scr, S.at[pl.ds(HS, 16), pl.ds(8, 32)], lsem.at[2]),
    ]
    for c in loads:
        c.start()

    @pl.when(gx == 0)
    def _():
        R[pl.ds(0, HR)] = jnp.zeros((HR, 48, 128), jnp.float32)
        S[pl.ds(0, HS)] = jnp.zeros((HS, 48, 128), jnp.float32)
        M[0] = jnp.zeros((48, 128), jnp.float32)

    @pl.when(gx == NGX - 1)
    def _():
        R[pl.ds(HR + 16, HR)] = jnp.zeros((HR, 48, 128), jnp.float32)
        S[pl.ds(HS + 16, HS)] = jnp.zeros((HS, 48, 128), jnp.float32)
        M[2] = jnp.zeros((48, 128), jnp.float32)

    def clear_rows(row):
        R[:, pl.ds(row, 8)] = jnp.zeros((28, 8, 128), jnp.float32)
        S[:, pl.ds(row, 8)] = jnp.zeros((24, 8, 128), jnp.float32)
        M[:, pl.ds(row, 8)] = jnp.zeros((3, 8, 128), jnp.float32)

    @pl.when(gy == 0)
    def _():
        clear_rows(0)

    @pl.when(gy == NGY - 1)
    def _():
        clear_rows(40)

    lane = lax.broadcasted_iota(jnp.int32, (8, 128), 1)
    loads[0].wait()
    entries = [act_s[0, q] for q in range(ACT)]
    count = jnp.int32(0)
    for e in entries:
        count = count + jnp.where(e >= 0, 1, 0)
    for w in range(2):
        number = lane // BLK + 8 * w
        own = jnp.zeros((8, 128), jnp.float32)
        for e in entries:
            own = jnp.where(number == e, 1.0, own)
        M[1, pl.ds(8 + 16 * w, 8)] = own
        M[1, pl.ds(16 + 16 * w, 8)] = own
    loads[1].wait()
    loads[2].wait()

    def prepare(p, carry):
        R[HR + p, pl.ds(8, 32)] = R[HR + p, pl.ds(8, 32)] * M[1, pl.ds(8, 32)]
        S[HS + p, pl.ds(8, 32)] = S[HS + p, pl.ds(8, 32)] - SIGMA
        return carry

    lax.fori_loop(0, 16, prepare, 0)

    pl.semaphore_wait(bar, 35)

    def pieces(i):
        dx, dy = NEIGHBOURS[i]
        rows = {0: (8, 8, 32), 1: (32, 0, 8), -1: (8, 40, 8)}[dy]
        out = []
        for n, (ref, h) in enumerate(((R, HR), (S, HS))):
            planes = {0: (h, h, 16), 1: (16, 0, h), -1: (h, h + 16, h)}[dx]
            out.append((ref.at[pl.ds(planes[0], planes[2]), pl.ds(rows[0], rows[2])],
                        ref.at[pl.ds(planes[1], planes[2]), pl.ds(rows[1], rows[2])], n))
        out.append((M.at[1, pl.ds(rows[0], rows[2])], M.at[1 - dx, pl.ds(rows[1], rows[2])], 2))
        return [pltpu.make_async_remote_copy(s, d, ssem.at[i, n], rsem.at[i, n],
                                             device_id=(gx + dx, gy + dy), device_id_type=MESH)
                for s, d, n in out]

    opposite = [NEIGHBOURS.index((-dx, -dy)) for dx, dy in NEIGHBOURS]
    for i, ok in enumerate(has):
        @pl.when(ok)
        def _():
            for c in pieces(i):
                c.start()
    for i in range(8):
        @pl.when(has[opposite[i]])
        def _():
            for c in pieces(i):
                c.wait_recv()

    lane48 = lax.broadcasted_iota(jnp.int32, (48, 128), 1)
    low1, low2 = lane48 < 1, lane48 < 2
    high1, high2 = lane48 > 126, lane48 > 125

    def zy_pass(src, count, tiles):
        first, rows = tiles

        def step(p, carry):
            v = src[p]
            p1 = jnp.where(low1, 0.0, pltpu.roll(v, 1, 1)) + jnp.where(high1, 0.0, pltpu.roll(v, 127, 1))
            p2 = jnp.where(low2, 0.0, pltpu.roll(v, 2, 1)) + jnp.where(high2, 0.0, pltpu.roll(v, 126, 1))
            MZ[p, pl.ds(8, 48)] = 66.0 * v + 26.0 * p1 + p2
            SZ[p, pl.ds(8, 48)] = 6.0 * v - 2.0 * p1 - p2

            def rows_at(ref, off):
                return ref[p, pl.ds(8 + first + off, rows)]

            s0 = rows_at(SZ, 0)
            s1 = rows_at(SZ, -1) + rows_at(SZ, 1)
            s2 = rows_at(SZ, -2) + rows_at(SZ, 2)
            m0 = rows_at(MZ, 0)
            m1 = rows_at(MZ, -1) + rows_at(MZ, 1)
            m2 = rows_at(MZ, -2) + rows_at(MZ, 2)
            IN[p, pl.ds(first, rows)] = (66.0 * s0 + 26.0 * s1 + s2) + (6.0 * m0 - 2.0 * m1 - m2)
            OUT[p, pl.ds(first, rows)] = 66.0 * m0 + 26.0 * m1 + m2
            return carry

        lax.fori_loop(0, count, step, 0)

    def x_value(p, src, smap, m, first, rows):
        def pick(ref, off):
            return ref[p + off, pl.ds(first, rows)]

        i1 = pick(IN, 1) + pick(IN, 3)
        i2 = pick(IN, 0) + pick(IN, 4)
        o1 = pick(OUT, 1) + pick(OUT, 3)
        o2 = pick(OUT, 0) + pick(OUT, 4)
        k = (66.0 * pick(IN, 2) + 26.0 * i1 + i2) + (6.0 * pick(OUT, 2) - 2.0 * o1 - o2)
        centre = src[p + 2, pl.ds(first, rows)]
        return m * (k * SCALE + S[p + smap, pl.ds(first, rows)] * centre), centre

    def fold(v):
        return (v[0:8] + v[8:16]) + (v[16:24] + v[24:32])

    def apply(src, dst, planes, halo, smap):
        zero = jnp.zeros((8, 128), jnp.float32)
        for lo, hi, dx in ((0, halo, 0), (halo, halo + 16, 1), (halo + 16, planes, 2)):
            def step(p, acc):
                value, centre = x_value(p, src, smap, M[dx], 0, 48)
                dst[p] = value
                if dx != 1:
                    return acc
                u, v = value[8:40], centre[8:40]
                return acc[0] + fold(v * u), acc[1] + fold(u * u), acc[2] + fold(u)

            out = lax.fori_loop(lo, hi, step, (zero, zero, zero))
            if dx == 1:
                sums = out
        return sums

    zero = jnp.zeros((8, 128), jnp.float32)

    def first_sums(p, acc):
        v = R[HR + p, pl.ds(8, 32)]
        return acc[0] + fold(v * v), acc[1] + fold(v)

    mu0, sum0 = lax.fori_loop(0, 16, first_sums, (zero, zero))
    zy_pass(R, 28, (0, 48))
    mu1, mu2, sum1 = apply(R, U1, 24, 4, 0)
    zy_pass(U1, 24, (0, 48))
    mu3, mu4, sum2 = apply(U1, U2, 20, 2, 2)
    zy_pass(U2, 20, (8, 32))

    def last(p, acc):
        value, centre = x_value(p, U2, 4, M[1, pl.ds(8, 32)], 8, 32)
        return acc + fold(value * centre)

    mu5 = lax.fori_loop(0, 16, last, zero)

    sub16 = lax.broadcasted_iota(jnp.int32, (16, 128), 0)
    lane16 = lax.broadcasted_iota(jnp.int32, (16, 128), 1)
    rows = jnp.zeros((16, 128), jnp.float32)
    for k, acc in enumerate((mu0, mu1, mu2, mu3, mu4, mu5, sum0, sum1, sum2)):
        rows = jnp.where(sub16 == k, jnp.sum(acc, axis=0, keepdims=True), rows)
    total = jnp.sum(rows, axis=1, keepdims=True)
    spread = jnp.where(lane16 == sub16, total, 0.0)
    values = jnp.sum(spread, axis=0, keepdims=True)
    lane1 = lax.broadcasted_iota(jnp.int32, (1, 128), 1)
    coarse = jnp.zeros((1, 128), jnp.float32)
    for k in range(6):
        coarse = jnp.where(lane1 == k, 1.5 * 2.0 ** (26 + k), coarse)
    rounded = (values + coarse) - coarse
    high = jnp.where(lane1 < 6, rounded, values)
    rest = jnp.where(lane1 < 6, values - rounded, 0.0)
    row = high + pltpu.roll(rest, 64, 1)
    row = jnp.where(lane1 == 9, count.astype(jnp.float32), row)

    pending = []

    ar1[gy] = row
    for j in (8, 7, 9, 6, 10, 5, 11, 4, 12, 3, 13, 2, 14, 1, 15):
        pltpu.make_async_remote_copy(
            ar1.at[gy], ar1.at[gy], asem.at[0], arsem.at[0],
            device_id=(gx, lax.rem(gy + j, NGY)), device_id_type=MESH).start()
    wait = pltpu.make_async_remote_copy(
        ar1.at[pl.ds(0, 15)], ar1.at[pl.ds(0, 15)], asem.at[0], arsem.at[0],
        device_id=(gx, lax.rem(gy + 1, NGY)), device_id_type=MESH)
    wait.wait_recv()
    pending.append(wait)
    row = jnp.sum(ar1[...], axis=0)

    ar2[6 + core] = row
    targets = [(off, c) for off in (-4, 3, -3, 2, -2, 1, -1) for c in (0, 1)]
    for off, c in targets:
        pltpu.make_async_remote_copy(
            ar2.at[6 + core], ar2.at[(3 - off) * 2 + core], asem.at[1], arsem.at[1],
            device_id=(at_z(off, c), gy), device_id_type=MESH).start()
    pltpu.make_async_remote_copy(
        ar2.at[6 + core], ar2.at[6 + core], asem.at[1], arsem.at[1],
        device_id=(at_z(0, 1 - core), gy), device_id_type=MESH).start()
    wait = pltpu.make_async_remote_copy(
        ar2.at[pl.ds(0, 15)], ar2.at[pl.ds(0, 15)], asem.at[1], arsem.at[1],
        device_id=(at_z(1, core), gy), device_id_type=MESH)
    wait.wait_recv()
    pending.append(wait)
    stage[...] = jnp.sum(ar2[...], axis=0)
    for slot, off in ((0, -4), (1, 4)):
        pltpu.make_async_remote_copy(
            stage, ar3.at[slot], asem.at[2], arsem.at[2],
            device_id=(at_z(off, core), gy), device_id_type=MESH).start()
    wait = pltpu.make_async_remote_copy(
        ar3, ar3, asem.at[2], arsem.at[2], device_id=(at_z(4, core), gy), device_id_type=MESH)
    wait.wait_recv()
    pending.append(wait)
    row = ar3[0] + ar3[1]

    goal = jnp.where(sub16 < 10, sub16, sub16 + 54)
    picked = jnp.sum(jnp.where(lane16 == goal, row, 0.0), axis=1, keepdims=True)
    value = [jnp.broadcast_to(picked[k:k + 1], (8, 128)) for k in range(16)]
    mu = [two_sum(value[k], value[10 + k]) for k in range(6)]
    c0, c1, c2 = cg_weights(mu)
    iso = (c0 * value[6] + c1 * value[7] + c2 * value[8]) / (value[9] * float(BLK ** 3))

    def tile5(v):
        return jnp.concatenate([v] * 5, axis=0)

    iso_out[...] = iso
    c0, c1, c2 = tile5(c0), tile5(c1), tile5(c2)

    def solve(p, carry):
        x_out[p] = c0 * R[HR + p, pl.ds(8, 40)] + c1 * U1[4 + p, pl.ds(8, 40)] + c2 * U2[2 + p, pl.ds(8, 40)]
        return carry

    lax.fori_loop(0, 17, solve, 0)

    for i, ok in enumerate(has):
        @pl.when(ok)
        def _():
            for c in pieces(i):
                c.wait_send()
    for c in pending:
        c.wait_send()


def crossing_kernel(x_ref, iso_ref, vis, ind_out, cross_out, G, W, BR, vis_s, sem):
    load = pltpu.make_async_copy(vis.at[0], vis_s, sem.at[0])
    load.start()
    store = pltpu.make_async_copy(x_ref.at[pl.ds(0, 16), pl.ds(0, 32)], ind_out, sem.at[1])
    store.start()
    lane = lax.broadcasted_iota(jnp.int32, (8, 128), 1)
    iso = jnp.concatenate([iso_ref[...]] * 5, axis=0)

    def squash(p, carry):
        G[p] = sigmoid4(x_ref[p] - iso)
        return carry

    lax.fori_loop(0, 17, squash, 0)
    BR[pl.ds(16 * 96, 96)] = jnp.zeros((96, 128), jnp.float32)

    lane32 = lax.broadcasted_iota(jnp.int32, (32, 128), 1)
    edge = lane32 == 127
    empty = sigmoid4(0.0 - iso[0:32])

    def weigh(p, carry):
        g = G[p, pl.ds(0, 32)]
        gx1 = G[p + 1, pl.ds(0, 32)]
        gy1 = G[p, pl.ds(1, 32)]
        gz1 = jnp.where(edge, empty, pltpu.roll(g, 127, 1))
        for e, other in enumerate((gx1, gy1, gz1)):
            h = crossing_weight(g, other)
            for w in range(2):
                base = (p // 4) * 128 + w * 64 + lax.rem(p, 4) * 16
                W[e, pl.ds(pl.multiple_of(base, 16), 16)] = h[16 * w:16 * w + 16]
        return carry

    lax.fori_loop(0, 16, weigh, 0)

    group = lane // BLK

    def regroup(b, carry):
        e = b // 8
        part = lax.rem(b, 8)
        w = lax.rem(b, 2)
        ib = part // 2
        vs = [W[e, pl.ds(part * 64 + j, 8, stride=8)] for j in range(8)]
        for bit in range(3):
            d = 1 << bit
            odd = (group // d) % 2 == 1
            new = list(vs)
            for j in range(8):
                if not j & d:
                    lo, hi = vs[j], vs[j + d]
                    new[j] = jnp.where(odd, pltpu.roll(hi, 16 * d, 1), lo)
                    new[j + d] = jnp.where(odd, hi, pltpu.roll(lo, 128 - 16 * d, 1))
            vs = new
        for t in range(8):
            base = (w * 8 + t) * 96 + e * 32 + ib * 8
            BR[pl.ds(pl.multiple_of(base, 8), 8)] = vs[t]
        return carry

    lax.fori_loop(0, 24, regroup, 0)

    load.wait()
    stores = []
    for q in range(VIS):
        n = vis_s[0, q]
        start = pl.multiple_of(jnp.where(n >= 0, n, 16) * 96, 8)
        stores.append(pltpu.make_async_copy(
            BR.at[pl.ds(start, 96)], cross_out.at[pl.ds(q * 96, 96)], sem.at[2 + q]))
        stores[-1].start()
    store.wait()
    for c in stores:
        c.wait()


def body(right_side, screening, active_blocks, visible_bricks):
    f32 = jnp.float32
    right_side, screening, active_blocks, visible_bricks = (
        pltpu.with_memory_space_constraint(v, pltpu.HBM)
        for v in (right_side, screening, active_blocks, visible_bricks))
    hbm = pl.BlockSpec(memory_space=pltpu.HBM)
    vmem = pl.BlockSpec(memory_space=pltpu.VMEM)
    x, iso = pl.pallas_call(
        solve_kernel,
        out_shape=(jax.ShapeDtypeStruct((17, 40, 128), f32), jax.ShapeDtypeStruct((8, 128), f32)),
        in_specs=[hbm] * 3,
        out_specs=(vmem, vmem),
        scratch_shapes=[
            pltpu.VMEM((28, 48, 128), f32),
            pltpu.VMEM((24, 48, 128), f32),
            pltpu.VMEM((3, 48, 128), f32),
            pltpu.VMEM((24, 48, 128), f32),
            pltpu.VMEM((20, 48, 128), f32),
            pltpu.VMEM((28, 64, 128), f32),
            pltpu.VMEM((28, 64, 128), f32),
            pltpu.VMEM((28, 48, 128), f32),
            pltpu.VMEM((28, 48, 128), f32),
            pltpu.SMEM((1, ACT), jnp.int32),
            pltpu.VMEM((16, 1, 128), f32),
            pltpu.VMEM((16, 1, 128), f32),
            pltpu.VMEM((2, 1, 128), f32),
            pltpu.VMEM((1, 128), f32),
            pltpu.SemaphoreType.DMA((3,)),
            pltpu.SemaphoreType.DMA((8, 3)),
            pltpu.SemaphoreType.DMA((8, 3)),
            pltpu.SemaphoreType.DMA((3,)),
            pltpu.SemaphoreType.DMA((3,)),
        ],
        compiler_params=pltpu.CompilerParams(
            collective_id=0, has_side_effects=True, vmem_limit_bytes=32 << 20),
    )(right_side, screening, active_blocks)
    indicator, crossing = pl.pallas_call(
        crossing_kernel,
        out_shape=(jax.ShapeDtypeStruct((16, 32, 128), f32), jax.ShapeDtypeStruct((VIS * 96, 128), f32)),
        in_specs=[vmem, vmem, hbm],
        out_specs=(hbm, hbm),
        scratch_shapes=[
            pltpu.VMEM((17, 40, 128), f32),
            pltpu.VMEM((3, 512, 128), f32),
            pltpu.VMEM((17 * 96, 128), f32),
            pltpu.SMEM((1, VIS), jnp.int32),
            pltpu.SemaphoreType.DMA((2 + VIS,)),
        ],
        compiler_params=pltpu.CompilerParams(vmem_limit_bytes=24 << 20),
    )(x, iso, visible_bricks)
    return indicator, crossing.reshape(VIS, 1, 3, BLK ** 3)


def solution(mesh):
    spec = P("gx", "gy", None)
    return jax.shard_map(
        body,
        mesh=mesh,
        in_specs=(spec, spec, spec, spec),
        out_specs=(spec, P("gx", "gy", None, None)),
        check_vma=False,
    )
```

time: 718 us -> 55.3 us (0.08)
  blocking collectives: 616 us -> 0 us
  Pallas kernels: 0 us -> 54.5 us
  starting transfers between devices: 38.4 us -> 0 us
  waiting for transfers between devices: 17.1 us -> 0 us
  other arithmetic: 12.3 us -> 0 us
  loops' own time: 11.8 us -> 0 us
  local copies, waits for them, and re-layouts: 11.3 us -> 0 us
  between operations: 9.04 us -> 0.64 us
    psum x6 -> x0, blocking collectives: 616 us -> none  [the longest x3 309 us: squares(): return lax.psum(jnp.sum(residual * residual), ('gx', 'gy'))]
    pallas_call x0 -> x2, Pallas kernels: none -> 54.5 us  [the longest x1 46.7 us: body(): pl.pallas_call(solve_kernel, out_shape=(jax.ShapeDtypeStruct((17, 40, 128...]
    ppermute x14 -> x0, starting transfers between devices: 38.4 us -> none  [the longest x6 21.7 us: with_halo(): lax.ppermute(lax.slice_in_dim(block, block.shape[dim] - width, None, axis...]
    ppermute x14 -> x0, waiting for transfers between devices: 17.1 us -> none  [the longest x6 17.1 us: with_halo(): lax.ppermute(lax.slice_in_dim(block, 0, width, axis=dim), axis, backward)]
    another operation x1 -> x0, loops' own time: 11.8 us -> none  [body(): weights = lax.map(brick_weights, bricks)]
  transfers between devices with their start and end apart: 14 -> 0, of which waited for: 6 -> 0; matrix products, arithmetic and copies ran while one was open for 0% -> 0% of each run, Pallas kernels for 0% -> 0%
where the time goes in v1:
time: 55.3 us; the launch traced here: 55.2 us
  Pallas kernels  54.5 us (99%)
  between operations  0.64 us (1%)
    pallas_call x1, Pallas kernels, body(): pl.pallas_call(solve_kernel, out_shape=(jax.ShapeDtypeStruct((17, 40, 128...  46.7 us
    pallas_call x1, Pallas kernels, body(): pl.pallas_call(crossing_kernel, out_shape=(jax.ShapeDtypeStruct((16, 32,...  7.81 us

profile of v1, /device:TPU:1, one launch (start us, length us, event | category | flops | bytes accessed | tf_op | source)
XLA Modules:
  0.0 55.2 jit_solution(17991855242590848673)
XLA Ops:
  0.6 46.7 %shard_map.59 = (f32[17,40,128]{2,1,0:T(8,128)S(1)}, f32[8,128]{1,0:T(8,128)S(1)}) custom-call(f32[16,32,128]{2,1,0:T(8,128)} %rhs.1, f32[16,32,128]{2,1,0:T(8,128)} %scr.1, s32[1,1,12]{2,1,0:T(1,128)} %act.1), custom_call_target="tpu_custom_call" | custom-call | tf_op jit(solution)/shard_map/pallas_call | solution.py:476
  47.4 7.8 %shard_map.60 = (f32[16,32,128]{2,1,0:T(8,128)}, f32[768,128]{1,0:T(8,128)}) custom-call(f32[17,40,128]{2,1,0:T(8,128)S(1)} %get-tuple-element.6.x_ref, f32[8,128]{1,0:T(8,128)S(1)} %get-tuple-element.7.iso_ref, s32[1,1,8]{2,1,0:T(1,128)} %vis.1), custom_call_target="tpu_custom_call" | custom-call | tf_op jit(solution)/shard_map/pallas_call | solution.py:505

commit v2 on v1

--- a/solution.py
+++ b/solution.py
@@ -202,7 +202,7 @@
         S[HS + p, pl.ds(8, 32)] = S[HS + p, pl.ds(8, 32)] - SIGMA
         return carry
 
-    lax.fori_loop(0, 16, prepare, 0)
+    lax.fori_loop(0, 16, prepare, 0, unroll=4)
 
     pl.semaphore_wait(bar, 35)
 
@@ -258,7 +258,7 @@
             OUT[p, pl.ds(first, rows)] = 66.0 * m0 + 26.0 * m1 + m2
             return carry
 
-        lax.fori_loop(0, count, step, 0)
+        lax.fori_loop(0, count, step, 0, unroll=4)
 
     def x_value(p, src, smap, m, first, rows):
         def pick(ref, off):
@@ -286,7 +286,7 @@
                 u, v = value[8:40], centre[8:40]
                 return acc[0] + fold(v * u), acc[1] + fold(u * u), acc[2] + fold(u)
 
-            out = lax.fori_loop(lo, hi, step, (zero, zero, zero))
+            out = lax.fori_loop(lo, hi, step, (zero, zero, zero), unroll=min(4, hi - lo))
             if dx == 1:
                 sums = out
         return sums
@@ -297,7 +297,7 @@
         v = R[HR + p, pl.ds(8, 32)]
         return acc[0] + fold(v * v), acc[1] + fold(v)
 
-    mu0, sum0 = lax.fori_loop(0, 16, first_sums, (zero, zero))
+    mu0, sum0 = lax.fori_loop(0, 16, first_sums, (zero, zero), unroll=4)
     zy_pass(R, 28, (0, 48))
     mu1, mu2, sum1 = apply(R, U1, 24, 4, 0)
     zy_pass(U1, 24, (0, 48))
@@ -308,7 +308,7 @@
         value, centre = x_value(p, U2, 4, M[1, pl.ds(8, 32)], 8, 32)
         return acc + fold(value * centre)
 
-    mu5 = lax.fori_loop(0, 16, last, zero)
+    mu5 = lax.fori_loop(0, 16, last, zero, unroll=4)
 
     sub16 = lax.broadcasted_iota(jnp.int32, (16, 128), 0)
     lane16 = lax.broadcasted_iota(jnp.int32, (16, 128), 1)
@@ -384,7 +384,7 @@
         x_out[p] = c0 * R[HR + p, pl.ds(8, 40)] + c1 * U1[4 + p, pl.ds(8, 40)] + c2 * U2[2 + p, pl.ds(8, 40)]
         return carry
 
-    lax.fori_loop(0, 17, solve, 0)
+    lax.fori_loop(0, 17, solve, 0, unroll=True)
 
     for i, ok in enumerate(has):
         @pl.when(ok)
@@ -403,65 +403,52 @@
     lane = lax.broadcasted_iota(jnp.int32, (8, 128), 1)
     iso = jnp.concatenate([iso_ref[...]] * 5, axis=0)
 
-    def squash(p, carry):
+    for p in range(17):
         G[p] = sigmoid4(x_ref[p] - iso)
-        return carry
-
-    lax.fori_loop(0, 17, squash, 0)
     BR[pl.ds(16 * 96, 96)] = jnp.zeros((96, 128), jnp.float32)
 
     lane32 = lax.broadcasted_iota(jnp.int32, (32, 128), 1)
     edge = lane32 == 127
     empty = sigmoid4(0.0 - iso[0:32])
-
-    def weigh(p, carry):
-        g = G[p, pl.ds(0, 32)]
-        gx1 = G[p + 1, pl.ds(0, 32)]
-        gy1 = G[p, pl.ds(1, 32)]
-        gz1 = jnp.where(edge, empty, pltpu.roll(g, 127, 1))
-        for e, other in enumerate((gx1, gy1, gz1)):
+    group = lane // BLK
+    odd = [(group // (1 << bit)) % 2 == 1 for bit in range(3)]
+    load.wait()
+    slots = []
+    for q in range(VIS):
+        n = vis_s[0, q]
+        slots.append(jnp.where(n >= 0, n, 16) * 96)
+    stores = [store]
+    for e in range(3):
+        for p in range(16):
+            g = G[p, pl.ds(0, 32)]
+            if e == 0:
+                other = G[p + 1, pl.ds(0, 32)]
+            elif e == 1:
+                other = G[p, pl.ds(1, 32)]
+            else:
+                other = jnp.where(edge, empty, pltpu.roll(g, 127, 1))
             h = crossing_weight(g, other)
             for w in range(2):
-                base = (p // 4) * 128 + w * 64 + lax.rem(p, 4) * 16
-                W[e, pl.ds(pl.multiple_of(base, 16), 16)] = h[16 * w:16 * w + 16]
-        return carry
-
-    lax.fori_loop(0, 16, weigh, 0)
-
-    group = lane // BLK
-
-    def regroup(b, carry):
-        e = b // 8
-        part = lax.rem(b, 8)
-        w = lax.rem(b, 2)
-        ib = part // 2
-        vs = [W[e, pl.ds(part * 64 + j, 8, stride=8)] for j in range(8)]
-        for bit in range(3):
-            d = 1 << bit
-            odd = (group // d) % 2 == 1
-            new = list(vs)
-            for j in range(8):
-                if not j & d:
-                    lo, hi = vs[j], vs[j + d]
-                    new[j] = jnp.where(odd, pltpu.roll(hi, 16 * d, 1), lo)
-                    new[j + d] = jnp.where(odd, hi, pltpu.roll(lo, 128 - 16 * d, 1))
-            vs = new
-        for t in range(8):
-            base = (w * 8 + t) * 96 + e * 32 + ib * 8
-            BR[pl.ds(pl.multiple_of(base, 8), 8)] = vs[t]
-        return carry
-
-    lax.fori_loop(0, 24, regroup, 0)
-
-    load.wait()
-    stores = []
-    for q in range(VIS):
-        n = vis_s[0, q]
-        start = pl.multiple_of(jnp.where(n >= 0, n, 16) * 96, 8)
-        stores.append(pltpu.make_async_copy(
-            BR.at[pl.ds(start, 96)], cross_out.at[pl.ds(q * 96, 96)], sem.at[2 + q]))
-        stores[-1].start()
-    store.wait()
+                W[e, pl.ds((p // 4) * 128 + w * 64 + p % 4 * 16, 16)] = h[16 * w:16 * w + 16]
+        for part in range(8):
+            w, ib = part % 2, part // 2
+            vs = [W[e, pl.ds(part * 64 + j, 8, stride=8)] for j in range(8)]
+            for bit in range(3):
+                d = 1 << bit
+                new = list(vs)
+                for j in range(8):
+                    if not j & d:
+                        lo, hi = vs[j], vs[j + d]
+                        new[j] = jnp.where(odd[bit], pltpu.roll(hi, 16 * d, 1), lo)
+                        new[j + d] = jnp.where(odd[bit], hi, pltpu.roll(lo, 128 - 16 * d, 1))
+                vs = new
+            for t in range(8):
+                BR[pl.ds((w * 8 + t) * 96 + e * 32 + ib * 8, 8)] = vs[t]
+        for q in range(VIS):
+            start = pl.multiple_of(slots[q] + e * 32, 8)
+            stores.append(pltpu.make_async_copy(
+                BR.at[pl.ds(start, 32)], cross_out.at[pl.ds(q * 96 + e * 32, 32)], sem.at[2 + q * 3 + e]))
+            stores[-1].start()
     for c in stores:
         c.wait()
 
@@ -512,7 +499,7 @@
             pltpu.VMEM((3, 512, 128), f32),
             pltpu.VMEM((17 * 96, 128), f32),
             pltpu.SMEM((1, VIS), jnp.int32),
-            pltpu.SemaphoreType.DMA((2 + VIS,)),
+            pltpu.SemaphoreType.DMA((2 + 3 * VIS,)),
         ],
         compiler_params=pltpu.CompilerParams(vmem_limit_bytes=24 << 20),
     )(x, iso, visible_bricks)

time: 55.3 us -> 46.8 us (0.85)
  Pallas kernels: 54.5 us -> 46 us
    pallas_call x1, Pallas kernels: 46.7 us -> 41.7 us  [body(): pl.pallas_call(solve_kernel, out_shape=(jax.ShapeDtypeStruct((17, 40, 128...]
    pallas_call x1, Pallas kernels: 7.81 us -> 4.25 us  [body(): pl.pallas_call(crossing_kernel, out_shape=(jax.ShapeDtypeStruct((16, 32,...]
where the time goes in v2:
time: 46.8 us; the launch traced here: 46.6 us
  Pallas kernels  46 us (98%)
  between operations  0.64 us (1%)
    pallas_call x1, Pallas kernels, body(): pl.pallas_call(solve_kernel, out_shape=(jax.ShapeDtypeStruct((17, 40, 128...  41.7 us
    pallas_call x1, Pallas kernels, body(): pl.pallas_call(crossing_kernel, out_shape=(jax.ShapeDtypeStruct((16, 32,...  4.25 us

profile of v2, /device:TPU:1, one launch (start us, length us, event | category | flops | bytes accessed | tf_op | source)
XLA Modules:
  0.0 46.6 jit_solution(6081983867917147849)
XLA Ops:
  0.6 41.7 %shard_map.59 = (f32[17,40,128]{2,1,0:T(8,128)S(1)}, f32[8,128]{1,0:T(8,128)S(1)}) custom-call(f32[16,32,128]{2,1,0:T(8,128)} %rhs.1, f32[16,32,128]{2,1,0:T(8,128)} %scr.1, s32[1,1,12]{2,1,0:T(1,128)} %act.1), custom_call_target="tpu_custom_call" | custom-call | tf_op jit(solution)/shard_map/pallas_call | solution.py:463
  42.4 4.2 %shard_map.60 = (f32[16,32,128]{2,1,0:T(8,128)}, f32[768,128]{1,0:T(8,128)}) custom-call(f32[17,40,128]{2,1,0:T(8,128)S(1)} %get-tuple-element.6.x_ref, f32[8,128]{1,0:T(8,128)S(1)} %get-tuple-element.7.iso_ref, s32[1,1,8]{2,1,0:T(1,128)} %vis.1), custom_call_target="tpu_custom_call" | custom-call | tf_op jit(solution)/shard_map/pallas_call | solution.py:492

commit v3 on v2

--- a/solution.py
+++ b/solution.py
@@ -115,28 +115,31 @@
 
 
 def solve_kernel(rhs, scr, act, x_out, iso_out,
-           R, S, M, U1, U2, MZ, SZ, IN, OUT, act_s, ar1, ar2, ar3, stage,
-           lsem, ssem, rsem, asem, arsem):
+           R, S, M, U1, U2, MZ, SZ, IN, OUT, act_s, ar1, ar2,
+                 lsem, ssem, rsem, asem, arsem, token):
     gx = lax.axis_index("gx")
     gy = lax.axis_index("gy")
     z = gx // 2
     core = lax.rem(gx, 2)
 
-    def at_z(off, c):
-        return lax.rem(z + off + NZ, NZ) * 2 + c
+    def at_z(off):
+        return lax.rem(z + off + NZ, NZ) * 2 + core
 
     bar = pltpu.get_barrier_semaphore()
 
     def tell(x, y):
         pl.semaphore_signal(bar, inc=1, device_id=(x, y), device_id_type=MESH)
 
-    tell(at_z(-4, core), gy)
-    for off in (4, -3, 3, -2, 2, -1, 1):
-        for c in (0, 1):
-            tell(at_z(off, c), gy)
-    tell(at_z(0, 1 - core), gy)
-    for j in range(1, NGY):
-        tell(gx, lax.rem(gy + j, NGY))
+    other_chip = lax.rem(gx + 2 * core - 1 + NGX, NGX)
+    for dy in (1, -1):
+        tell(other_chip, lax.rem(gy + dy + NGY, NGY))
+    tell(other_chip, gy)
+    for j in (1, 15, 10, 6, 9, 7, 11, 5, 8, 2, 14, 13, 3, 12, 4):
+        for c in (1 - core, core):
+            tell(2 * z + c, lax.rem(gy + j, NGY))
+    tell(2 * z + 1 - core, gy)
+    for off in (4, -4, 3, -3, 2, -2, 1, -1):
+        tell(at_z(off), gy)
     has = []
     for dx, dy in NEIGHBOURS:
         ok = None
@@ -144,10 +147,6 @@
             [gy < NGY - 1] if dy == 1 else []) + ([gy > 0] if dy == -1 else []):
             ok = cond if ok is None else jnp.logical_and(ok, cond)
         has.append(ok)
-    for dx, dy in NEIGHBOURS:
-        if dx and dy:
-            tell(lax.rem(gx + dx + NGX, NGX), lax.rem(gy + dy + NGY, NGY))
-
     loads = [
         pltpu.make_async_copy(act.at[0], act_s, lsem.at[0]),
         pltpu.make_async_copy(rhs, R.at[pl.ds(HR, 16), pl.ds(8, 32)], lsem.at[1]),
@@ -160,26 +159,26 @@
     def _():
         R[pl.ds(0, HR)] = jnp.zeros((HR, 48, 128), jnp.float32)
         S[pl.ds(0, HS)] = jnp.zeros((HS, 48, 128), jnp.float32)
-        M[0] = jnp.zeros((48, 128), jnp.float32)
+        M[0] = jnp.zeros((4, 128), jnp.float32)
 
     @pl.when(gx == NGX - 1)
     def _():
         R[pl.ds(HR + 16, HR)] = jnp.zeros((HR, 48, 128), jnp.float32)
         S[pl.ds(HS + 16, HS)] = jnp.zeros((HS, 48, 128), jnp.float32)
-        M[2] = jnp.zeros((48, 128), jnp.float32)
-
-    def clear_rows(row):
+        M[2] = jnp.zeros((4, 128), jnp.float32)
+
+    def clear_rows(row, kind):
         R[:, pl.ds(row, 8)] = jnp.zeros((28, 8, 128), jnp.float32)
         S[:, pl.ds(row, 8)] = jnp.zeros((24, 8, 128), jnp.float32)
-        M[:, pl.ds(row, 8)] = jnp.zeros((3, 8, 128), jnp.float32)
+        M[:, pl.ds(kind, 1)] = jnp.zeros((3, 1, 128), jnp.float32)
 
     @pl.when(gy == 0)
     def _():
-        clear_rows(0)
+        clear_rows(0, 0)
 
     @pl.when(gy == NGY - 1)
     def _():
-        clear_rows(40)
+        clear_rows(40, 3)
 
     lane = lax.broadcasted_iota(jnp.int32, (8, 128), 1)
     loads[0].wait()
@@ -192,44 +191,73 @@
         own = jnp.zeros((8, 128), jnp.float32)
         for e in entries:
             own = jnp.where(number == e, 1.0, own)
-        M[1, pl.ds(8 + 16 * w, 8)] = own
-        M[1, pl.ds(16 + 16 * w, 8)] = own
+        M[1, pl.ds(1 + w, 1)] = own[0:1]
     loads[1].wait()
     loads[2].wait()
 
+    def mask_rows(dx, kinds):
+        tiles = [jnp.broadcast_to(M[dx, pl.ds(k, 1)], (8, 128)) for k in range(4)]
+        return jnp.concatenate([tiles[k] for k in kinds], axis=0)
+
+    own = mask_rows(1, (1, 1, 2, 2))
+
     def prepare(p, carry):
-        R[HR + p, pl.ds(8, 32)] = R[HR + p, pl.ds(8, 32)] * M[1, pl.ds(8, 32)]
+        R[HR + p, pl.ds(8, 32)] = R[HR + p, pl.ds(8, 32)] * own
         S[HS + p, pl.ds(8, 32)] = S[HS + p, pl.ds(8, 32)] - SIGMA
         return carry
 
     lax.fori_loop(0, 16, prepare, 0, unroll=4)
 
-    pl.semaphore_wait(bar, 35)
-
-    def pieces(i):
+    pl.semaphore_wait(bar, 42)
+    for off in (4, -4):
+        pl.semaphore_signal(token, inc=1, device_id=(at_z(off), gy), device_id_type=MESH)
+
+    def pieces(i, which):
         dx, dy = NEIGHBOURS[i]
-        rows = {0: (8, 8, 32), 1: (32, 0, 8), -1: (8, 40, 8)}[dy]
         out = []
-        for n, (ref, h) in enumerate(((R, HR), (S, HS))):
-            planes = {0: (h, h, 16), 1: (16, 0, h), -1: (h, h + 16, h)}[dx]
-            out.append((ref.at[pl.ds(planes[0], planes[2]), pl.ds(rows[0], rows[2])],
-                        ref.at[pl.ds(planes[1], planes[2]), pl.ds(rows[1], rows[2])], n))
-        out.append((M.at[1, pl.ds(rows[0], rows[2])], M.at[1 - dx, pl.ds(rows[1], rows[2])], 2))
-        return [pltpu.make_async_remote_copy(s, d, ssem.at[i, n], rsem.at[i, n],
-                                             device_id=(gx + dx, gy + dy), device_id_type=MESH)
-                for s, d, n in out]
+        for n in which:
+            if n == 2:
+                first, size = {0: (1, 2), 1: (2, 1), -1: (1, 1)}[dy]
+                src = M.at[1, pl.ds(first, size)]
+                dst = M.at[1 - dx, pl.ds({0: 1, 1: 0, -1: 3}[dy], size)]
+            else:
+                ref, h = ((R, HR), (S, HS))[n]
+                planes = {0: (h, h, 16), 1: (16, 0, h), -1: (h, h + 16, h)}[dx]
+                rows = {0: (8, 8, 32), 1: (40 - h, 8 - h, h), -1: (8, 40, h)}[dy]
+                src = ref.at[pl.ds(planes[0], planes[2]), pl.ds(rows[0], rows[2])]
+                dst = ref.at[pl.ds(planes[1], planes[2]), pl.ds(rows[1], rows[2])]
+            out.append(pltpu.make_async_remote_copy(
+                src, dst, ssem.at[i, n], rsem.at[i, n],
+                device_id=(gx + dx, gy + dy), device_id_type=MESH))
+        return out
 
     opposite = [NEIGHBOURS.index((-dx, -dy)) for dx, dy in NEIGHBOURS]
-    for i, ok in enumerate(has):
-        @pl.when(ok)
-        def _():
-            for c in pieces(i):
-                c.start()
-    for i in range(8):
-        @pl.when(has[opposite[i]])
-        def _():
-            for c in pieces(i):
-                c.wait_recv()
+
+    def receive(which):
+        for i in range(8):
+            @pl.when(has[opposite[i]])
+            def _():
+                for c in pieces(i, which):
+                    c.wait_recv()
+
+    for which in ((0,), (2, 1)):
+        for i, ok in enumerate(has):
+            @pl.when(ok)
+            def _():
+                for c in pieces(i, which):
+                    c.start()
+
+    zero = jnp.zeros((8, 128), jnp.float32)
+
+    def fold(v):
+        return (v[0:8] + v[8:16]) + (v[16:24] + v[24:32])
+
+    def first_sums(p, acc):
+        v = R[HR + p, pl.ds(8, 32)]
+        return acc[0] + fold(v * v), acc[1] + fold(v)
+
+    mu0, sum0 = lax.fori_loop(0, 16, first_sums, (zero, zero), unroll=4)
+    receive((0,))
 
     lane48 = lax.broadcasted_iota(jnp.int32, (48, 128), 1)
     low1, low2 = lane48 < 1, lane48 < 2
@@ -272,14 +300,12 @@
         centre = src[p + 2, pl.ds(first, rows)]
         return m * (k * SCALE + S[p + smap, pl.ds(first, rows)] * centre), centre
 
-    def fold(v):
-        return (v[0:8] + v[8:16]) + (v[16:24] + v[24:32])
-
     def apply(src, dst, planes, halo, smap):
-        zero = jnp.zeros((8, 128), jnp.float32)
         for lo, hi, dx in ((0, halo, 0), (halo, halo + 16, 1), (halo + 16, planes, 2)):
+            m = mask_rows(dx, (0, 1, 1, 2, 2, 3))
+
             def step(p, acc):
-                value, centre = x_value(p, src, smap, M[dx], 0, 48)
+                value, centre = x_value(p, src, smap, m, 0, 48)
                 dst[p] = value
                 if dx != 1:
                     return acc
@@ -291,21 +317,15 @@
                 sums = out
         return sums
 
-    zero = jnp.zeros((8, 128), jnp.float32)
-
-    def first_sums(p, acc):
-        v = R[HR + p, pl.ds(8, 32)]
-        return acc[0] + fold(v * v), acc[1] + fold(v)
-
-    mu0, sum0 = lax.fori_loop(0, 16, first_sums, (zero, zero), unroll=4)
     zy_pass(R, 28, (0, 48))
+    receive((2, 1))
     mu1, mu2, sum1 = apply(R, U1, 24, 4, 0)
     zy_pass(U1, 24, (0, 48))
     mu3, mu4, sum2 = apply(U1, U2, 20, 2, 2)
     zy_pass(U2, 20, (8, 32))
 
     def last(p, acc):
-        value, centre = x_value(p, U2, 4, M[1, pl.ds(8, 32)], 8, 32)
+        value, centre = x_value(p, U2, 4, own, 8, 32)
         return acc + fold(value * centre)
 
     mu5 = lax.fori_loop(0, 16, last, zero, unroll=4)
@@ -329,43 +349,33 @@
     row = jnp.where(lane1 == 9, count.astype(jnp.float32), row)
 
     pending = []
-
-    ar1[gy] = row
-    for j in (8, 7, 9, 6, 10, 5, 11, 4, 12, 3, 13, 2, 14, 1, 15):
-        pltpu.make_async_remote_copy(
-            ar1.at[gy], ar1.at[gy], asem.at[0], arsem.at[0],
-            device_id=(gx, lax.rem(gy + j, NGY)), device_id_type=MESH).start()
+    mine = gy * 2 + core
+    ar1[mine] = row
+    for j in (10, 6, 9, 7, 11, 5, 8, 2, 14, 13, 3, 1, 15, 12, 4, 0):
+        for c in (1 - core, core):
+            if j == 0 and c is core:
+                continue
+            pltpu.make_async_remote_copy(
+                ar1.at[mine], ar1.at[mine], asem.at[0], arsem.at[0],
+                device_id=(2 * z + c, lax.rem(gy + j, NGY)), device_id_type=MESH).start()
     wait = pltpu.make_async_remote_copy(
-        ar1.at[pl.ds(0, 15)], ar1.at[pl.ds(0, 15)], asem.at[0], arsem.at[0],
-        device_id=(gx, lax.rem(gy + 1, NGY)), device_id_type=MESH)
+        ar1.at[pl.ds(0, 31)], ar1.at[pl.ds(0, 31)], asem.at[0], arsem.at[0],
+        device_id=(2 * z + 1 - core, gy), device_id_type=MESH)
     wait.wait_recv()
     pending.append(wait)
-    row = jnp.sum(ar1[...], axis=0)
-
-    ar2[6 + core] = row
-    targets = [(off, c) for off in (-4, 3, -3, 2, -2, 1, -1) for c in (0, 1)]
-    for off, c in targets:
+
+    ar2[z] = jnp.sum(ar1[...], axis=0)
+    pl.semaphore_wait(token, 2)
+    for off in (8, 7, -7, 6, -6, 5, -5, 4, -4, 3, -3, 2, -2, 1, -1):
         pltpu.make_async_remote_copy(
-            ar2.at[6 + core], ar2.at[(3 - off) * 2 + core], asem.at[1], arsem.at[1],
-            device_id=(at_z(off, c), gy), device_id_type=MESH).start()
-    pltpu.make_async_remote_copy(
-        ar2.at[6 + core], ar2.at[6 + core], asem.at[1], arsem.at[1],
-        device_id=(at_z(0, 1 - core), gy), device_id_type=MESH).start()
+            ar2.at[z], ar2.at[z], asem.at[1], arsem.at[1],
+            device_id=(at_z(off), gy), device_id_type=MESH).start()
     wait = pltpu.make_async_remote_copy(
         ar2.at[pl.ds(0, 15)], ar2.at[pl.ds(0, 15)], asem.at[1], arsem.at[1],
-        device_id=(at_z(1, core), gy), device_id_type=MESH)
+        device_id=(at_z(1), gy), device_id_type=MESH)
     wait.wait_recv()
     pending.append(wait)
-    stage[...] = jnp.sum(ar2[...], axis=0)
-    for slot, off in ((0, -4), (1, 4)):
-        pltpu.make_async_remote_copy(
-            stage, ar3.at[slot], asem.at[2], arsem.at[2],
-            device_id=(at_z(off, core), gy), device_id_type=MESH).start()
-    wait = pltpu.make_async_remote_copy(
-        ar3, ar3, asem.at[2], arsem.at[2], device_id=(at_z(4, core), gy), device_id_type=MESH)
-    wait.wait_recv()
-    pending.append(wait)
-    row = ar3[0] + ar3[1]
+    row = jnp.sum(ar2[...], axis=0)
 
     goal = jnp.where(sub16 < 10, sub16, sub16 + 54)
     picked = jnp.sum(jnp.where(lane16 == goal, row, 0.0), axis=1, keepdims=True)
@@ -389,7 +399,7 @@
     for i, ok in enumerate(has):
         @pl.when(ok)
         def _():
-            for c in pieces(i):
+            for c in pieces(i, (0, 1, 2)):
                 c.wait_send()
     for c in pending:
         c.wait_send()
@@ -468,7 +478,7 @@
         scratch_shapes=[
             pltpu.VMEM((28, 48, 128), f32),
             pltpu.VMEM((24, 48, 128), f32),
-            pltpu.VMEM((3, 48, 128), f32),
+            pltpu.VMEM((3, 4, 128), f32),
             pltpu.VMEM((24, 48, 128), f32),
             pltpu.VMEM((20, 48, 128), f32),
             pltpu.VMEM((28, 64, 128), f32),
@@ -476,15 +486,14 @@
             pltpu.VMEM((28, 48, 128), f32),
             pltpu.VMEM((28, 48, 128), f32),
             pltpu.SMEM((1, ACT), jnp.int32),
+            pltpu.VMEM((32, 1, 128), f32),
             pltpu.VMEM((16, 1, 128), f32),
-            pltpu.VMEM((16, 1, 128), f32),
-            pltpu.VMEM((2, 1, 128), f32),
-            pltpu.VMEM((1, 128), f32),
             pltpu.SemaphoreType.DMA((3,)),
             pltpu.SemaphoreType.DMA((8, 3)),
             pltpu.SemaphoreType.DMA((8, 3)),
-            pltpu.SemaphoreType.DMA((3,)),
-            pltpu.SemaphoreType.DMA((3,)),
+            pltpu.SemaphoreType.DMA((2,)),
+            pltpu.SemaphoreType.DMA((2,)),
+            pltpu.SemaphoreType.REGULAR,
         ],
         compiler_params=pltpu.CompilerParams(
             collective_id=0, has_side_effects=True, vmem_limit_bytes=32 << 20),

time: 46.8 us -> 42.2 us (0.902)
  Pallas kernels: 46 us -> 41.5 us
    pallas_call x1, Pallas kernels: 41.7 us -> 37.2 us  [body(): pl.pallas_call(solve_kernel, out_shape=(jax.ShapeDtypeStruct((17, 40, 128...]
where the time goes in v3:
time: 42.2 us; the launch traced here: 42.1 us
  Pallas kernels  41.5 us (98%)
  between operations  0.64 us (2%)
    pallas_call x1, Pallas kernels, body(): pl.pallas_call(solve_kernel, out_shape=(jax.ShapeDtypeStruct((17, 40, 128...  37.2 us
    pallas_call x1, Pallas kernels, body(): pl.pallas_call(crossing_kernel, out_shape=(jax.ShapeDtypeStruct((16, 32,...  4.25 us

profile of v3, /device:TPU:1, one launch (start us, length us, event | category | flops | bytes accessed | tf_op | source)
XLA Modules:
  0.0 42.1 jit_solution(7166435319384399371)
XLA Ops:
  0.6 37.2 %shard_map.59 = (f32[17,40,128]{2,1,0:T(8,128)S(1)}, f32[8,128]{1,0:T(8,128)S(1)}) custom-call(f32[16,32,128]{2,1,0:T(8,128)} %rhs.1, f32[16,32,128]{2,1,0:T(8,128)} %scr.1, s32[1,1,12]{2,1,0:T(1,128)} %act.1), custom_call_target="tpu_custom_call" | custom-call | tf_op jit(solution)/shard_map/pallas_call | solution.py:473
  37.8 4.2 %shard_map.60 = (f32[16,32,128]{2,1,0:T(8,128)}, f32[768,128]{1,0:T(8,128)}) custom-call(f32[17,40,128]{2,1,0:T(8,128)S(1)} %get-tuple-element.6.x_ref, f32[8,128]{1,0:T(8,128)S(1)} %get-tuple-element.7.iso_ref, s32[1,1,8]{2,1,0:T(1,128)} %vis.1), custom_call_target="tpu_custom_call" | custom-call | tf_op jit(solution)/shard_map/pallas_call | solution.py:501

commit v4 on v3

--- a/solution.py
+++ b/solution.py
@@ -286,7 +286,7 @@
             OUT[p, pl.ds(first, rows)] = 66.0 * m0 + 26.0 * m1 + m2
             return carry
 
-        lax.fori_loop(0, count, step, 0, unroll=4)
+        lax.fori_loop(0, count, step, 0, unroll=True)
 
     def x_value(p, src, smap, m, first, rows):
         def pick(ref, off):
@@ -312,7 +312,7 @@
                 u, v = value[8:40], centre[8:40]
                 return acc[0] + fold(v * u), acc[1] + fold(u * u), acc[2] + fold(u)
 
-            out = lax.fori_loop(lo, hi, step, (zero, zero, zero), unroll=min(4, hi - lo))
+            out = lax.fori_loop(lo, hi, step, (zero, zero, zero), unroll=True)
             if dx == 1:
                 sums = out
         return sums
@@ -328,7 +328,7 @@
         value, centre = x_value(p, U2, 4, own, 8, 32)
         return acc + fold(value * centre)
 
-    mu5 = lax.fori_loop(0, 16, last, zero, unroll=4)
+    mu5 = lax.fori_loop(0, 16, last, zero, unroll=True)
 
     sub16 = lax.broadcasted_iota(jnp.int32, (16, 128), 0)
     lane16 = lax.broadcasted_iota(jnp.int32, (16, 128), 1)
@@ -440,20 +440,23 @@
             h = crossing_weight(g, other)
             for w in range(2):
                 W[e, pl.ds((p // 4) * 128 + w * 64 + p % 4 * 16, 16)] = h[16 * w:16 * w + 16]
-        for part in range(8):
-            w, ib = part % 2, part // 2
-            vs = [W[e, pl.ds(part * 64 + j, 8, stride=8)] for j in range(8)]
+        for first in range(0, 8, 4):
+            parts = range(first, first + 4)
+            vs = {}
+            for part in parts:
+                vs[part] = [W[e, pl.ds(part * 64 + (-j) % 8, 8, stride=8)] for j in range(8)]
+            for part in parts:
+                vs[part] = [v if j == 0 else pltpu.roll(v, 16 * ((-j) % 8), 1) for j, v in enumerate(vs[part])]
             for bit in range(3):
-                d = 1 << bit
-                new = list(vs)
-                for j in range(8):
-                    if not j & d:
-                        lo, hi = vs[j], vs[j + d]
-                        new[j] = jnp.where(odd[bit], pltpu.roll(hi, 16 * d, 1), lo)
-                        new[j + d] = jnp.where(odd[bit], hi, pltpu.roll(lo, 128 - 16 * d, 1))
-                vs = new
-            for t in range(8):
-                BR[pl.ds((w * 8 + t) * 96 + e * 32 + ib * 8, 8)] = vs[t]
+                for part in parts:
+                    old = vs[part]
+                    vs[part] = [jnp.where(odd[bit], old[(t - (1 << bit)) % 8], old[t]) for t in range(8)]
+            for part in parts:
+                vs[part] = [v if t == 0 else pltpu.roll(v, 128 - 16 * t, 1) for t, v in enumerate(vs[part])]
+            for part in parts:
+                w, ib = part % 2, part // 2
+                for t in range(8):
+                    BR[pl.ds((w * 8 + t) * 96 + e * 32 + ib * 8, 8)] = vs[part][t]
         for q in range(VIS):
             start = pl.multiple_of(slots[q] + e * 32, 8)
             stores.append(pltpu.make_async_copy(

time: 42.2 us -> 38.6 us (0.915)
  Pallas kernels: 41.5 us -> 37.8 us
    pallas_call x1, Pallas kernels: 4.25 us -> 2.31 us  [body(): pl.pallas_call(crossing_kernel, out_shape=(jax.ShapeDtypeStruct((16, 32,...]
    pallas_call x1, Pallas kernels: 37.2 us -> 35.5 us  [body(): pl.pallas_call(solve_kernel, out_shape=(jax.ShapeDtypeStruct((17, 40, 128...]
where the time goes in v4:
time: 38.6 us; the launch traced here: 38.4 us
  Pallas kernels  37.8 us (98%)
  between operations  0.64 us (2%)
    pallas_call x1, Pallas kernels, body(): pl.pallas_call(solve_kernel, out_shape=(jax.ShapeDtypeStruct((17, 40, 128...  35.5 us
    pallas_call x1, Pallas kernels, body(): pl.pallas_call(crossing_kernel, out_shape=(jax.ShapeDtypeStruct((16, 32,...  2.31 us

profile of v4, /device:TPU:1, one launch (start us, length us, event | category | flops | bytes accessed | tf_op | source)
XLA Modules:
  0.0 38.4 jit_solution(5668739479107758013)
XLA Ops:
  0.6 35.5 %shard_map.59 = (f32[17,40,128]{2,1,0:T(8,128)S(1)}, f32[8,128]{1,0:T(8,128)S(1)}) custom-call(f32[16,32,128]{2,1,0:T(8,128)} %rhs.1, f32[16,32,128]{2,1,0:T(8,128)} %scr.1, s32[1,1,12]{2,1,0:T(1,128)} %act.1), custom_call_target="tpu_custom_call" | custom-call | tf_op jit(solution)/shard_map/pallas_call | solution.py:476
  36.1 2.3 %shard_map.60 = (f32[16,32,128]{2,1,0:T(8,128)}, f32[768,128]{1,0:T(8,128)}) custom-call(f32[17,40,128]{2,1,0:T(8,128)S(1)} %get-tuple-element.6.x_ref, f32[8,128]{1,0:T(8,128)S(1)} %get-tuple-element.7.iso_ref, s32[1,1,8]{2,1,0:T(1,128)} %vis.1), custom_call_target="tpu_custom_call" | custom-call | tf_op jit(solution)/shard_map/pallas_call | solution.py:504

commit v5 on v4

--- a/solution.py
+++ b/solution.py
@@ -115,7 +115,7 @@
 
 
 def solve_kernel(rhs, scr, act, x_out, iso_out,
-           R, S, M, U1, U2, MZ, SZ, IN, OUT, act_s, ar1, ar2,
+           R, S, M, U1, U2, MZ, SZ, MZ2, SZ2, IN, OUT, act_s, ar1, ar2,
                  lsem, ssem, rsem, asem, arsem, token):
     gx = lax.axis_index("gx")
     gy = lax.axis_index("gy")
@@ -248,87 +248,134 @@
                     c.start()
 
     zero = jnp.zeros((8, 128), jnp.float32)
-
-    def fold(v):
-        return (v[0:8] + v[8:16]) + (v[16:24] + v[24:32])
-
-    def first_sums(p, acc):
-        v = R[HR + p, pl.ds(8, 32)]
-        return acc[0] + fold(v * v), acc[1] + fold(v)
-
-    mu0, sum0 = lax.fori_loop(0, 16, first_sums, (zero, zero), unroll=4)
+    sub = lax.broadcasted_iota(jnp.int32, (8, 128), 0)
+
+    lanes = lax.broadcasted_iota(jnp.int32, (48, 128), 1)
+
+    def z_stage(src, row, mz, sz, out_row, p, rows):
+        v = src[p, pl.ds(row, rows)]
+        at = lanes[0:rows]
+        p1 = jnp.where(at < 1, 0.0, pltpu.roll(v, 1, 1)) + jnp.where(at > 126, 0.0, pltpu.roll(v, 127, 1))
+        p2 = jnp.where(at < 2, 0.0, pltpu.roll(v, 2, 1)) + jnp.where(at > 125, 0.0, pltpu.roll(v, 126, 1))
+        mz[p, pl.ds(out_row, rows)] = 66.0 * v + 26.0 * p1 + p2
+        sz[p, pl.ds(out_row, rows)] = 6.0 * v - 2.0 * p1 - p2
+
+    def y_stage(mz, sz, row, p, out_row, rows):
+        def at(ref, off):
+            return ref[p, pl.ds(row + off, rows)]
+
+        s0 = at(sz, 0)
+        s1 = at(sz, -1) + at(sz, 1)
+        s2 = at(sz, -2) + at(sz, 2)
+        m0 = at(mz, 0)
+        m1 = at(mz, -1) + at(mz, 1)
+        m2 = at(mz, -2) + at(mz, 2)
+        IN[p, pl.ds(out_row, rows)] = (66.0 * s0 + 26.0 * s1 + s2) + (6.0 * m0 - 2.0 * m1 - m2)
+        OUT[p, pl.ds(out_row, rows)] = 66.0 * m0 + 26.0 * m1 + m2
+
+    def x_stage(p, row, rows, m, scr_rows, src, src_row):
+        def at(ref, off):
+            return ref[p + off, pl.ds(row, rows)]
+
+        i1 = at(IN, 1) + at(IN, 3)
+        i2 = at(IN, 0) + at(IN, 4)
+        o1 = at(OUT, 1) + at(OUT, 3)
+        o2 = at(OUT, 0) + at(OUT, 4)
+        k = (66.0 * at(IN, 2) + 26.0 * i1 + i2) + (6.0 * at(OUT, 2) - 2.0 * o1 - o2)
+        centre = src[p + 2, pl.ds(src_row, rows)]
+        return m * (k * SCALE + scr_rows * centre), centre
+
+    def total_of(acc, terms):
+        return tuple(x + y for x, y in zip(acc, terms))
+
+    def own_terms(value, centre, first, tiles):
+        terms = []
+        for prod in (value * centre, value * value, value):
+            t = [prod[8 * k:8 * k + 8] for k in range(tiles)]
+            if first is None:
+                terms.append((t[0] + t[1]) + t[2])
+            elif tiles == 2:
+                terms.append(jnp.where(sub >= first, t[0], t[1]))
+            else:
+                terms.append((jnp.where(sub >= first, t[0], t[4]) + t[1]) + (t[2] + t[3]))
+        return terms
+
+    def mask_from(dx, base):
+        k = [jnp.broadcast_to(M[dx, pl.ds(j, 1)], (8, 128)) for j in range(4)]
+        cut = sub >= -base
+        return jnp.concatenate([jnp.where(cut, k[1], k[0]), k[1], jnp.where(cut, k[2], k[1]), k[2],
+                                jnp.where(cut, k[3], k[2])], axis=0)
+
+    mu0, sum0 = zero, zero
+    for p in range(HR, HR + 16):
+        z_stage(R, 8, MZ, SZ, 16, p, 32)
+        v = R[p, pl.ds(8, 32)]
+        w = v * v
+        mu0 = mu0 + ((w[0:8] + w[8:16]) + (w[16:24] + w[24:32]))
+        sum0 = sum0 + ((v[0:8] + v[8:16]) + (v[16:24] + v[24:32]))
+    for p in range(HR, HR + 16):
+        y_stage(MZ, SZ, 20, p, 8, 24)
+    middle = jnp.concatenate([own[0:8], jnp.where(sub >= 4, own[16:24], own[0:8]), own[16:24]], axis=0)
+    acc = (zero, zero, zero)
+    for p in range(6, 18):
+        value, centre = x_stage(p, 8, 24, middle, S[p, pl.ds(12, 24)], R, 12)
+        U1[p, pl.ds(8, 24)] = value
+        acc = total_of(acc, own_terms(value, centre, None, 3))
+
     receive((0,))
-
-    lane48 = lax.broadcasted_iota(jnp.int32, (48, 128), 1)
-    low1, low2 = lane48 < 1, lane48 < 2
-    high1, high2 = lane48 > 126, lane48 > 125
-
-    def zy_pass(src, count, tiles):
-        first, rows = tiles
-
-        def step(p, carry):
-            v = src[p]
-            p1 = jnp.where(low1, 0.0, pltpu.roll(v, 1, 1)) + jnp.where(high1, 0.0, pltpu.roll(v, 127, 1))
-            p2 = jnp.where(low2, 0.0, pltpu.roll(v, 2, 1)) + jnp.where(high2, 0.0, pltpu.roll(v, 126, 1))
-            MZ[p, pl.ds(8, 48)] = 66.0 * v + 26.0 * p1 + p2
-            SZ[p, pl.ds(8, 48)] = 6.0 * v - 2.0 * p1 - p2
-
-            def rows_at(ref, off):
-                return ref[p, pl.ds(8 + first + off, rows)]
-
-            s0 = rows_at(SZ, 0)
-            s1 = rows_at(SZ, -1) + rows_at(SZ, 1)
-            s2 = rows_at(SZ, -2) + rows_at(SZ, 2)
-            m0 = rows_at(MZ, 0)
-            m1 = rows_at(MZ, -1) + rows_at(MZ, 1)
-            m2 = rows_at(MZ, -2) + rows_at(MZ, 2)
-            IN[p, pl.ds(first, rows)] = (66.0 * s0 + 26.0 * s1 + s2) + (6.0 * m0 - 2.0 * m1 - m2)
-            OUT[p, pl.ds(first, rows)] = 66.0 * m0 + 26.0 * m1 + m2
-            return carry
-
-        lax.fori_loop(0, count, step, 0, unroll=True)
-
-    def x_value(p, src, smap, m, first, rows):
-        def pick(ref, off):
-            return ref[p + off, pl.ds(first, rows)]
-
-        i1 = pick(IN, 1) + pick(IN, 3)
-        i2 = pick(IN, 0) + pick(IN, 4)
-        o1 = pick(OUT, 1) + pick(OUT, 3)
-        o2 = pick(OUT, 0) + pick(OUT, 4)
-        k = (66.0 * pick(IN, 2) + 26.0 * i1 + i2) + (6.0 * pick(OUT, 2) - 2.0 * o1 - o2)
-        centre = src[p + 2, pl.ds(first, rows)]
-        return m * (k * SCALE + S[p + smap, pl.ds(first, rows)] * centre), centre
-
-    def apply(src, dst, planes, halo, smap):
-        for lo, hi, dx in ((0, halo, 0), (halo, halo + 16, 1), (halo + 16, planes, 2)):
-            m = mask_rows(dx, (0, 1, 1, 2, 2, 3))
-
-            def step(p, acc):
-                value, centre = x_value(p, src, smap, m, 0, 48)
-                dst[p] = value
-                if dx != 1:
-                    return acc
-                u, v = value[8:40], centre[8:40]
-                return acc[0] + fold(v * u), acc[1] + fold(u * u), acc[2] + fold(u)
-
-            out = lax.fori_loop(lo, hi, step, (zero, zero, zero), unroll=True)
+    for p in range(28):
+        if HR <= p < HR + 16:
+            z_stage(R, 0, MZ, SZ, 8, p, 8)
+            z_stage(R, 40, MZ, SZ, 48, p, 8)
+        else:
+            z_stage(R, 0, MZ, SZ, 8, p, 48)
+    for p in range(28):
+        if HR <= p < HR + 16:
+            y_stage(MZ, SZ, 12, p, 0, 8)
+            y_stage(MZ, SZ, 44, p, 32, 8)
+        else:
+            y_stage(MZ, SZ, 12, p, 0, 40)
+    receive((2, 1))
+    masks = [mask_from(dx, -4) for dx in range(3)]
+    for p in range(24):
+        dx = 0 if p < 4 else 1 if p < 20 else 2
+        if 6 <= p < 18:
+            low, c_low = x_stage(p, 0, 8, masks[1][0:8], S[p, pl.ds(4, 8)], R, 4)
+            high, c_high = x_stage(p, 32, 8, masks[1][32:40], S[p, pl.ds(36, 8)], R, 36)
+            U1[p, pl.ds(0, 8)] = low
+            U1[p, pl.ds(32, 8)] = high
+            acc = total_of(acc, own_terms(jnp.concatenate([low, high], axis=0),
+                                          jnp.concatenate([c_low, c_high], axis=0), 4, 2))
+        else:
+            value, centre = x_stage(p, 0, 40, masks[dx], S[p, pl.ds(4, 40)], R, 4)
+            U1[p, pl.ds(0, 40)] = value
             if dx == 1:
-                sums = out
-        return sums
-
-    zy_pass(R, 28, (0, 48))
-    receive((2, 1))
-    mu1, mu2, sum1 = apply(R, U1, 24, 4, 0)
-    zy_pass(U1, 24, (0, 48))
-    mu3, mu4, sum2 = apply(U1, U2, 20, 2, 2)
-    zy_pass(U2, 20, (8, 32))
-
-    def last(p, acc):
-        value, centre = x_value(p, U2, 4, own, 8, 32)
-        return acc + fold(value * centre)
-
-    mu5 = lax.fori_loop(0, 16, last, zero, unroll=True)
+                acc = total_of(acc, own_terms(value, centre, 4, 5))
+    mu1, mu2, sum1 = acc
+
+    for p in range(24):
+        z_stage(U1, 0, MZ2, SZ2, 8, p, 40)
+    for p in range(24):
+        y_stage(MZ2, SZ2, 10, p, 0, 40)
+    masks = [mask_from(dx, -2) for dx in range(3)]
+    acc = (zero, zero, zero)
+    for p in range(20):
+        dx = 0 if p < 2 else 1 if p < 18 else 2
+        value, centre = x_stage(p, 0, 40, masks[dx], S[p + 2, pl.ds(6, 40)], U1, 2)
+        U2[p, pl.ds(0, 40)] = value
+        if dx == 1:
+            acc = total_of(acc, own_terms(value, centre, 2, 5))
+    mu3, mu4, sum2 = acc
+
+    for p in range(20):
+        z_stage(U2, 0, MZ, SZ, 8, p, 40)
+    for p in range(20):
+        y_stage(MZ, SZ, 10, p, 0, 32)
+    mu5 = zero
+    for p in range(16):
+        value, centre = x_stage(p, 0, 32, own, S[p + 4, pl.ds(8, 32)], U2, 2)
+        w = value * centre
+        mu5 = mu5 + ((w[0:8] + w[8:16]) + (w[16:24] + w[24:32]))
 
     sub16 = lax.broadcasted_iota(jnp.int32, (16, 128), 0)
     lane16 = lax.broadcasted_iota(jnp.int32, (16, 128), 1)
@@ -391,7 +438,7 @@
     c0, c1, c2 = tile5(c0), tile5(c1), tile5(c2)
 
     def solve(p, carry):
-        x_out[p] = c0 * R[HR + p, pl.ds(8, 40)] + c1 * U1[4 + p, pl.ds(8, 40)] + c2 * U2[2 + p, pl.ds(8, 40)]
+        x_out[p] = c0 * R[HR + p, pl.ds(8, 40)] + c1 * U1[4 + p, pl.ds(4, 40)] + c2 * U2[2 + p, pl.ds(2, 40)]
         return carry
 
     lax.fori_loop(0, 17, solve, 0, unroll=True)
@@ -486,6 +533,8 @@
             pltpu.VMEM((20, 48, 128), f32),
             pltpu.VMEM((28, 64, 128), f32),
             pltpu.VMEM((28, 64, 128), f32),
+            pltpu.VMEM((24, 56, 128), f32),
+            pltpu.VMEM((24, 56, 128), f32),
             pltpu.VMEM((28, 48, 128), f32),
             pltpu.VMEM((28, 48, 128), f32),
             pltpu.SMEM((1, ACT), jnp.int32),

time: 38.6 us -> 37.8 us (0.979)
  Pallas kernels: 37.8 us -> 37 us
    pallas_call x1, Pallas kernels: 35.5 us -> 34.7 us  [body(): pl.pallas_call(solve_kernel, out_shape=(jax.ShapeDtypeStruct((17, 40, 128...]
where the time goes in v5:
time: 37.8 us; the launch traced here: 37.7 us
  Pallas kernels  37 us (98%)
  between operations  0.64 us (2%)
    pallas_call x1, Pallas kernels, body(): pl.pallas_call(solve_kernel, out_shape=(jax.ShapeDtypeStruct((17, 40, 128...  34.7 us
    pallas_call x1, Pallas kernels, body(): pl.pallas_call(crossing_kernel, out_shape=(jax.ShapeDtypeStruct((16, 32,...  2.31 us

profile of v5, /device:TPU:1, one launch (start us, length us, event | category | flops | bytes accessed | tf_op | source)
XLA Modules:
  0.0 37.7 jit_solution(5210920963600603973)
XLA Ops:
  0.6 34.7 %shard_map.59 = (f32[17,40,128]{2,1,0:T(8,128)S(1)}, f32[8,128]{1,0:T(8,128)S(1)}) custom-call(f32[16,32,128]{2,1,0:T(8,128)} %rhs.1, f32[16,32,128]{2,1,0:T(8,128)} %scr.1, s32[1,1,12]{2,1,0:T(1,128)} %act.1), custom_call_target="tpu_custom_call" | custom-call | tf_op jit(solution)/shard_map/pallas_call | solution.py:523
  35.4 2.3 %shard_map.60 = (f32[16,32,128]{2,1,0:T(8,128)}, f32[768,128]{1,0:T(8,128)}) custom-call(f32[17,40,128]{2,1,0:T(8,128)S(1)} %get-tuple-element.6.x_ref, f32[8,128]{1,0:T(8,128)S(1)} %get-tuple-element.7.iso_ref, s32[1,1,8]{2,1,0:T(1,128)} %vis.1), custom_call_target="tpu_custom_call" | custom-call | tf_op jit(solution)/shard_map/pallas_call | solution.py:553

commit v6 on v5

--- a/solution.py
+++ b/solution.py
@@ -106,6 +106,12 @@
     return c0, c1, c2
 
 
+def tree(parts):
+    while len(parts) > 1:
+        parts = [a + b for a, b in zip(parts[::2], parts[1::2])]
+    return parts[0]
+
+
 def sigmoid4(v):
     return 1.0 / (1.0 + jnp.exp(-4.0 * v))
 
@@ -115,7 +121,7 @@
 
 
 def solve_kernel(rhs, scr, act, x_out, iso_out,
-           R, S, M, U1, U2, MZ, SZ, MZ2, SZ2, IN, OUT, act_s, ar1, ar2,
+           R, S, M, U1, U2, MZ, SZ, MZ2, SZ2, TA, TB, act_s, ar1, ar2,
                  lsem, ssem, rsem, asem, arsem, token):
     gx = lax.axis_index("gx")
     gy = lax.axis_index("gy")
@@ -124,6 +130,14 @@
 
     def at_z(off):
         return lax.rem(z + off + NZ, NZ) * 2 + core
+
+    loads = [
+        pltpu.make_async_copy(act.at[0], act_s, lsem.at[0]),
+        pltpu.make_async_copy(rhs, R.at[pl.ds(HR, 16), pl.ds(8, 32)], lsem.at[1]),
+        pltpu.make_async_copy(scr, S.at[pl.ds(HS, 16), pl.ds(8, 32)], lsem.at[2]),
+    ]
+    for c in loads:
+        c.start()
 
     bar = pltpu.get_barrier_semaphore()
 
@@ -147,14 +161,6 @@
             [gy < NGY - 1] if dy == 1 else []) + ([gy > 0] if dy == -1 else []):
             ok = cond if ok is None else jnp.logical_and(ok, cond)
         has.append(ok)
-    loads = [
-        pltpu.make_async_copy(act.at[0], act_s, lsem.at[0]),
-        pltpu.make_async_copy(rhs, R.at[pl.ds(HR, 16), pl.ds(8, 32)], lsem.at[1]),
-        pltpu.make_async_copy(scr, S.at[pl.ds(HS, 16), pl.ds(8, 32)], lsem.at[2]),
-    ]
-    for c in loads:
-        c.start()
-
     @pl.when(gx == 0)
     def _():
         R[pl.ds(0, HR)] = jnp.zeros((HR, 48, 128), jnp.float32)
@@ -233,8 +239,12 @@
 
     opposite = [NEIGHBOURS.index((-dx, -dy)) for dx, dy in NEIGHBOURS]
 
-    def receive(which):
+    def receive(which, kinds=(0, 1, 2)):
         for i in range(8):
+            dx, dy = NEIGHBOURS[i]
+            if (2 if dx and dy else 0 if dx else 1) not in kinds:
+                continue
+
             @pl.when(has[opposite[i]])
             def _():
                 for c in pieces(i, which):
@@ -260,30 +270,28 @@
         mz[p, pl.ds(out_row, rows)] = 66.0 * v + 26.0 * p1 + p2
         sz[p, pl.ds(out_row, rows)] = 6.0 * v - 2.0 * p1 - p2
 
-    def y_stage(mz, sz, row, p, out_row, rows):
-        def at(ref, off):
-            return ref[p, pl.ds(row + off, rows)]
-
-        s0 = at(sz, 0)
-        s1 = at(sz, -1) + at(sz, 1)
-        s2 = at(sz, -2) + at(sz, 2)
-        m0 = at(mz, 0)
-        m1 = at(mz, -1) + at(mz, 1)
-        m2 = at(mz, -2) + at(mz, 2)
-        IN[p, pl.ds(out_row, rows)] = (66.0 * s0 + 26.0 * s1 + s2) + (6.0 * m0 - 2.0 * m1 - m2)
-        OUT[p, pl.ds(out_row, rows)] = 66.0 * m0 + 26.0 * m1 + m2
-
-    def x_stage(p, row, rows, m, scr_rows, src, src_row):
+    def x_stage(mz, sz, to, p, row, rows):
         def at(ref, off):
             return ref[p + off, pl.ds(row, rows)]
 
-        i1 = at(IN, 1) + at(IN, 3)
-        i2 = at(IN, 0) + at(IN, 4)
-        o1 = at(OUT, 1) + at(OUT, 3)
-        o2 = at(OUT, 0) + at(OUT, 4)
-        k = (66.0 * at(IN, 2) + 26.0 * i1 + i2) + (6.0 * at(OUT, 2) - 2.0 * o1 - o2)
+        s1 = at(sz, 1) + at(sz, 3)
+        s2 = at(sz, 0) + at(sz, 4)
+        m1 = at(mz, 1) + at(mz, 3)
+        m2 = at(mz, 0) + at(mz, 4)
+        m0 = at(mz, 2)
+        one = (66.0 * at(sz, 2) + 26.0 * s1 + s2) + (6.0 * m0 - 2.0 * m1 - m2)
+        two = 66.0 * m0 + 26.0 * m1 + m2
+        to[0, p, pl.ds(row, rows)] = (66.0 * SCALE) * one + (6.0 * SCALE) * two
+        to[1, p, pl.ds(row, rows)] = (26.0 * SCALE) * one - (2.0 * SCALE) * two
+        to[2, p, pl.ds(row, rows)] = SCALE * (one - two)
+
+    def y_stage(to, p, row, rows, m, scr_rows, src, src_row):
+        def at(k, off):
+            return to[k, p, pl.ds(row + off, rows)]
+
+        k = at(0, 0) + ((at(1, -1) + at(1, 1)) + (at(2, -2) + at(2, 2)))
         centre = src[p + 2, pl.ds(src_row, rows)]
-        return m * (k * SCALE + scr_rows * centre), centre
+        return m * (k + scr_rows * centre), centre
 
     def total_of(acc, terms):
         return tuple(x + y for x, y in zip(acc, terms))
@@ -313,82 +321,92 @@
         w = v * v
         mu0 = mu0 + ((w[0:8] + w[8:16]) + (w[16:24] + w[24:32]))
         sum0 = sum0 + ((v[0:8] + v[8:16]) + (v[16:24] + v[24:32]))
-    for p in range(HR, HR + 16):
-        y_stage(MZ, SZ, 20, p, 8, 24)
+    for p in range(6, 18):
+        x_stage(MZ, SZ, TA, p, 16, 32)
     middle = jnp.concatenate([own[0:8], jnp.where(sub >= 4, own[16:24], own[0:8]), own[16:24]], axis=0)
     acc = (zero, zero, zero)
     for p in range(6, 18):
-        value, centre = x_stage(p, 8, 24, middle, S[p, pl.ds(12, 24)], R, 12)
+        value, centre = y_stage(TA, p, 20, 24, middle, S[p, pl.ds(12, 24)], R, 12)
         U1[p, pl.ds(8, 24)] = value
         acc = total_of(acc, own_terms(value, centre, None, 3))
 
-    receive((0,))
-    for p in range(28):
-        if HR <= p < HR + 16:
-            z_stage(R, 0, MZ, SZ, 8, p, 8)
-            z_stage(R, 40, MZ, SZ, 48, p, 8)
-        else:
-            z_stage(R, 0, MZ, SZ, 8, p, 48)
-    for p in range(28):
-        if HR <= p < HR + 16:
-            y_stage(MZ, SZ, 12, p, 0, 8)
-            y_stage(MZ, SZ, 44, p, 32, 8)
-        else:
-            y_stage(MZ, SZ, 12, p, 0, 40)
+    halo = [p for p in range(28) if not HR <= p < HR + 16]
+    outer = [p for p in range(24) if not 6 <= p < 18]
+    receive((0,), (0,))
+    for p in halo:
+        z_stage(R, 8, MZ, SZ, 16, p, 32)
+    for p in outer:
+        x_stage(MZ, SZ, TA, p, 16, 32)
+    receive((0,), (1,))
+    for p in range(HR, HR + 16):
+        z_stage(R, 0, MZ, SZ, 8, p, 8)
+        z_stage(R, 40, MZ, SZ, 48, p, 8)
+    for p in range(6, 18):
+        x_stage(MZ, SZ, TA, p, 8, 8)
+        x_stage(MZ, SZ, TA, p, 48, 8)
+    receive((0,), (2,))
+    for p in halo:
+        z_stage(R, 0, MZ, SZ, 8, p, 8)
+        z_stage(R, 40, MZ, SZ, 48, p, 8)
+    for p in outer:
+        x_stage(MZ, SZ, TA, p, 8, 8)
+        x_stage(MZ, SZ, TA, p, 48, 8)
     receive((2, 1))
     masks = [mask_from(dx, -4) for dx in range(3)]
     for p in range(24):
         dx = 0 if p < 4 else 1 if p < 20 else 2
         if 6 <= p < 18:
-            low, c_low = x_stage(p, 0, 8, masks[1][0:8], S[p, pl.ds(4, 8)], R, 4)
-            high, c_high = x_stage(p, 32, 8, masks[1][32:40], S[p, pl.ds(36, 8)], R, 36)
+            low, c_low = y_stage(TA, p, 12, 8, masks[1][0:8], S[p, pl.ds(4, 8)], R, 4)
+            high, c_high = y_stage(TA, p, 44, 8, masks[1][32:40], S[p, pl.ds(36, 8)], R, 36)
             U1[p, pl.ds(0, 8)] = low
             U1[p, pl.ds(32, 8)] = high
             acc = total_of(acc, own_terms(jnp.concatenate([low, high], axis=0),
                                           jnp.concatenate([c_low, c_high], axis=0), 4, 2))
         else:
-            value, centre = x_stage(p, 0, 40, masks[dx], S[p, pl.ds(4, 40)], R, 4)
+            value, centre = y_stage(TA, p, 12, 40, masks[dx], S[p, pl.ds(4, 40)], R, 4)
             U1[p, pl.ds(0, 40)] = value
             if dx == 1:
                 acc = total_of(acc, own_terms(value, centre, 4, 5))
     mu1, mu2, sum1 = acc
 
-    for p in range(24):
+    for p in range(0, 24):
         z_stage(U1, 0, MZ2, SZ2, 8, p, 40)
-    for p in range(24):
-        y_stage(MZ2, SZ2, 10, p, 0, 40)
+    for p in range(20):
+        x_stage(MZ2, SZ2, TB, p, 8, 40)
     masks = [mask_from(dx, -2) for dx in range(3)]
     acc = (zero, zero, zero)
     for p in range(20):
         dx = 0 if p < 2 else 1 if p < 18 else 2
-        value, centre = x_stage(p, 0, 40, masks[dx], S[p + 2, pl.ds(6, 40)], U1, 2)
+        value, centre = y_stage(TB, p, 10, 40, masks[dx], S[p + 2, pl.ds(6, 40)], U1, 2)
         U2[p, pl.ds(0, 40)] = value
         if dx == 1:
             acc = total_of(acc, own_terms(value, centre, 2, 5))
     mu3, mu4, sum2 = acc
 
-    for p in range(20):
+    for p in range(0, 20):
         z_stage(U2, 0, MZ, SZ, 8, p, 40)
-    for p in range(20):
-        y_stage(MZ, SZ, 10, p, 0, 32)
-    mu5 = zero
     for p in range(16):
-        value, centre = x_stage(p, 0, 32, own, S[p + 4, pl.ds(8, 32)], U2, 2)
-        w = value * centre
-        mu5 = mu5 + ((w[0:8] + w[8:16]) + (w[16:24] + w[24:32]))
-
+        x_stage(MZ, SZ, TA, p, 8, 40)
     sub16 = lax.broadcasted_iota(jnp.int32, (16, 128), 0)
     lane16 = lax.broadcasted_iota(jnp.int32, (16, 128), 1)
+    lane1 = lax.broadcasted_iota(jnp.int32, (1, 128), 1)
     rows = jnp.zeros((16, 128), jnp.float32)
-    for k, acc in enumerate((mu0, mu1, mu2, mu3, mu4, mu5, sum0, sum1, sum2)):
+    for k, acc in ((0, mu0), (1, mu1), (2, mu2), (3, mu3), (4, mu4), (6, sum0), (7, sum1), (8, sum2)):
         rows = jnp.where(sub16 == k, jnp.sum(acc, axis=0, keepdims=True), rows)
     total = jnp.sum(rows, axis=1, keepdims=True)
     spread = jnp.where(lane16 == sub16, total, 0.0)
     values = jnp.sum(spread, axis=0, keepdims=True)
-    lane1 = lax.broadcasted_iota(jnp.int32, (1, 128), 1)
     coarse = jnp.zeros((1, 128), jnp.float32)
     for k in range(6):
         coarse = jnp.where(lane1 == k, 1.5 * 2.0 ** (26 + k), coarse)
+    mu5 = zero
+    for p in range(16):
+        value, centre = y_stage(TA, p, 10, 32, own, S[p + 4, pl.ds(8, 32)], U2, 2)
+        w = value * centre
+        mu5 = mu5 + ((w[0:8] + w[8:16]) + (w[16:24] + w[24:32]))
+
+    last = jnp.sum(jnp.sum(mu5, axis=0, keepdims=True), axis=1, keepdims=True)
+    values = jnp.where(lane1 == 5, last, values)
     rounded = (values + coarse) - coarse
     high = jnp.where(lane1 < 6, rounded, values)
     rest = jnp.where(lane1 < 6, values - rounded, 0.0)
@@ -411,7 +429,7 @@
     wait.wait_recv()
     pending.append(wait)
 
-    ar2[z] = jnp.sum(ar1[...], axis=0)
+    ar2[z] = tree([ar1[j] for j in range(32)])
     pl.semaphore_wait(token, 2)
     for off in (8, 7, -7, 6, -6, 5, -5, 4, -4, 3, -3, 2, -2, 1, -1):
         pltpu.make_async_remote_copy(
@@ -422,7 +440,7 @@
         device_id=(at_z(1), gy), device_id_type=MESH)
     wait.wait_recv()
     pending.append(wait)
-    row = jnp.sum(ar2[...], axis=0)
+    row = tree([ar2[j] for j in range(16)])
 
     goal = jnp.where(sub16 < 10, sub16, sub16 + 54)
     picked = jnp.sum(jnp.where(lane16 == goal, row, 0.0), axis=1, keepdims=True)
@@ -535,8 +553,8 @@
             pltpu.VMEM((28, 64, 128), f32),
             pltpu.VMEM((24, 56, 128), f32),
             pltpu.VMEM((24, 56, 128), f32),
-            pltpu.VMEM((28, 48, 128), f32),
-            pltpu.VMEM((28, 48, 128), f32),
+            pltpu.VMEM((3, 24, 64, 128), f32),
+            pltpu.VMEM((3, 20, 56, 128), f32),
             pltpu.SMEM((1, ACT), jnp.int32),
             pltpu.VMEM((32, 1, 128), f32),
             pltpu.VMEM((16, 1, 128), f32),

time: 37.8 us -> 37.5 us (level)
  no operation moved by 1% of the time
where the time goes in v6:
time: 37.5 us; the launch traced here: 37.3 us
  Pallas kernels  36.7 us (98%)
  between operations  0.64 us (2%)
    pallas_call x1, Pallas kernels, body(): pl.pallas_call(solve_kernel, out_shape=(jax.ShapeDtypeStruct((17, 40, 128...  34.4 us
    pallas_call x1, Pallas kernels, body(): pl.pallas_call(crossing_kernel, out_shape=(jax.ShapeDtypeStruct((16, 32,...  2.31 us

profile of v6, /device:TPU:1, one launch (start us, length us, event | category | flops | bytes accessed | tf_op | source)
XLA Modules:
  0.0 37.3 jit_solution(8882126281799592322)
XLA Ops:
  0.6 34.4 %shard_map.59 = (f32[17,40,128]{2,1,0:T(8,128)S(1)}, f32[8,128]{1,0:T(8,128)S(1)}) custom-call(f32[16,32,128]{2,1,0:T(8,128)} %rhs.1, f32[16,32,128]{2,1,0:T(8,128)} %scr.1, s32[1,1,12]{2,1,0:T(1,128)} %act.1), custom_call_target="tpu_custom_call" | custom-call | tf_op jit(solution)/shard_map/pallas_call | solution.py:541
  35.0 2.3 %shard_map.60 = (f32[16,32,128]{2,1,0:T(8,128)}, f32[768,128]{1,0:T(8,128)}) custom-call(f32[17,40,128]{2,1,0:T(8,128)S(1)} %get-tuple-element.6.x_ref, f32[8,128]{1,0:T(8,128)S(1)} %get-tuple-element.7.iso_ref, s32[1,1,8]{2,1,0:T(1,128)} %vis.1), custom_call_target="tpu_custom_call" | custom-call | tf_op jit(solution)/shard_map/pallas_call | solution.py:571

commit v7 on v6

--- a/solution.py
+++ b/solution.py
@@ -144,16 +144,14 @@
     def tell(x, y):
         pl.semaphore_signal(bar, inc=1, device_id=(x, y), device_id_type=MESH)
 
-    other_chip = lax.rem(gx + 2 * core - 1 + NGX, NGX)
-    for dy in (1, -1):
-        tell(other_chip, lax.rem(gy + dy + NGY, NGY))
-    tell(other_chip, gy)
-    for j in (1, 15, 10, 6, 9, 7, 11, 5, 8, 2, 14, 13, 3, 12, 4):
-        for c in (1 - core, core):
-            tell(2 * z + c, lax.rem(gy + j, NGY))
-    tell(2 * z + 1 - core, gy)
-    for off in (4, -4, 3, -3, 2, -2, 1, -1):
-        tell(at_z(off), gy)
+    def along_x(off):
+        return lax.rem(gx + off + NGX, NGX)
+
+    def along_y(off):
+        return lax.rem(gy + off + NGY, NGY)
+
+    for dx, dy in NEIGHBOURS:
+        tell(along_x(dx), along_y(dy))
     has = []
     for dx, dy in NEIGHBOURS:
         ok = None
@@ -214,9 +212,15 @@
 
     lax.fori_loop(0, 16, prepare, 0, unroll=4)
 
-    pl.semaphore_wait(bar, 42)
-    for off in (4, -4):
-        pl.semaphore_signal(token, inc=1, device_id=(at_z(off), gy), device_id_type=MESH)
+    pl.semaphore_wait(bar, 8)
+
+    def vouch(k):
+        for off in (1 << k, -(1 << k)):
+            pl.semaphore_signal(token.at[k], inc=1, device_id=(along_x(off), gy), device_id_type=MESH)
+            if k < 3:
+                pl.semaphore_signal(token.at[k], inc=1, device_id=(gx, along_y(off)), device_id_type=MESH)
+
+    vouch(0)
 
     def pieces(i, which):
         dx, dy = NEIGHBOURS[i]
@@ -332,6 +336,12 @@
 
     halo = [p for p in range(28) if not HR <= p < HR + 16]
     outer = [p for p in range(24) if not 6 <= p < 18]
+    for p in range(6, 18):
+        z_stage(U1, 8, MZ2, SZ2, 16, p, 24)
+    for p in range(6, 14):
+        x_stage(MZ2, SZ2, TB, p, 16, 24)
+    pl.semaphore_wait(token.at[0], 4)
+    vouch(1)
     receive((0,), (0,))
     for p in halo:
         z_stage(R, 8, MZ, SZ, 16, p, 32)
@@ -345,6 +355,8 @@
         x_stage(MZ, SZ, TA, p, 8, 8)
         x_stage(MZ, SZ, TA, p, 48, 8)
     receive((0,), (2,))
+    pl.semaphore_wait(token.at[1], 4)
+    vouch(2)
     for p in halo:
         z_stage(R, 0, MZ, SZ, 8, p, 8)
         z_stage(R, 40, MZ, SZ, 48, p, 8)
@@ -369,10 +381,18 @@
                 acc = total_of(acc, own_terms(value, centre, 4, 5))
     mu1, mu2, sum1 = acc
 
-    for p in range(0, 24):
-        z_stage(U1, 0, MZ2, SZ2, 8, p, 40)
+    for p in range(24):
+        if 6 <= p < 18:
+            z_stage(U1, 0, MZ2, SZ2, 8, p, 8)
+            z_stage(U1, 32, MZ2, SZ2, 40, p, 8)
+        else:
+            z_stage(U1, 0, MZ2, SZ2, 8, p, 40)
     for p in range(20):
-        x_stage(MZ2, SZ2, TB, p, 8, 40)
+        if 6 <= p < 14:
+            x_stage(MZ2, SZ2, TB, p, 8, 8)
+            x_stage(MZ2, SZ2, TB, p, 40, 8)
+        else:
+            x_stage(MZ2, SZ2, TB, p, 8, 40)
     masks = [mask_from(dx, -2) for dx in range(3)]
     acc = (zero, zero, zero)
     for p in range(20):
@@ -415,6 +435,7 @@
 
     pending = []
     mine = gy * 2 + core
+    pl.semaphore_wait(token.at[2], 4)
     ar1[mine] = row
     for j in (10, 6, 9, 7, 11, 5, 8, 2, 14, 13, 3, 1, 15, 12, 4, 0):
         for c in (1 - core, core):
@@ -426,15 +447,22 @@
     wait = pltpu.make_async_remote_copy(
         ar1.at[pl.ds(0, 31)], ar1.at[pl.ds(0, 31)], asem.at[0], arsem.at[0],
         device_id=(2 * z + 1 - core, gy), device_id_type=MESH)
+    vouch(3)
+    for i, ok in enumerate(has):
+        @pl.when(ok)
+        def _():
+            for c in pieces(i, (0, 1, 2)):
+                c.wait_send()
     wait.wait_recv()
     pending.append(wait)
 
     ar2[z] = tree([ar1[j] for j in range(32)])
-    pl.semaphore_wait(token, 2)
+    pl.semaphore_wait(token.at[3], 2)
     for off in (8, 7, -7, 6, -6, 5, -5, 4, -4, 3, -3, 2, -2, 1, -1):
         pltpu.make_async_remote_copy(
             ar2.at[z], ar2.at[z], asem.at[1], arsem.at[1],
             device_id=(at_z(off), gy), device_id_type=MESH).start()
+    pending.pop().wait_send()
     wait = pltpu.make_async_remote_copy(
         ar2.at[pl.ds(0, 15)], ar2.at[pl.ds(0, 15)], asem.at[1], arsem.at[1],
         device_id=(at_z(1), gy), device_id_type=MESH)
@@ -461,11 +489,6 @@
 
     lax.fori_loop(0, 17, solve, 0, unroll=True)
 
-    for i, ok in enumerate(has):
-        @pl.when(ok)
-        def _():
-            for c in pieces(i, (0, 1, 2)):
-                c.wait_send()
     for c in pending:
         c.wait_send()
 
@@ -563,7 +586,7 @@
             pltpu.SemaphoreType.DMA((8, 3)),
             pltpu.SemaphoreType.DMA((2,)),
             pltpu.SemaphoreType.DMA((2,)),
-            pltpu.SemaphoreType.REGULAR,
+            pltpu.SemaphoreType.REGULAR((4,)),
         ],
         compiler_params=pltpu.CompilerParams(
             collective_id=0, has_side_effects=True, vmem_limit_bytes=32 << 20),

time: 37.5 us -> 37.3 us (level)
  no operation moved by 1% of the time
where the time goes in v7:
time: 37.3 us; the launch traced here: 37.2 us
  Pallas kernels  36.5 us (98%)
  between operations  0.64 us (2%)
    pallas_call x1, Pallas kernels, body(): pl.pallas_call(solve_kernel, out_shape=(jax.ShapeDtypeStruct((17, 40, 128...  34.2 us
    pallas_call x1, Pallas kernels, body(): pl.pallas_call(crossing_kernel, out_shape=(jax.ShapeDtypeStruct((16, 32,...  2.31 us

profile of v7, /device:TPU:1, one launch (start us, length us, event | category | flops | bytes accessed | tf_op | source)
XLA Modules:
  0.0 37.2 jit_solution(8162177440432126101)
XLA Ops:
  0.6 34.2 %shard_map.59 = (f32[17,40,128]{2,1,0:T(8,128)S(1)}, f32[8,128]{1,0:T(8,128)S(1)}) custom-call(f32[16,32,128]{2,1,0:T(8,128)} %rhs.1, f32[16,32,128]{2,1,0:T(8,128)} %scr.1, s32[1,1,12]{2,1,0:T(1,128)} %act.1), custom_call_target="tpu_custom_call" | custom-call | tf_op jit(solution)/shard_map/pallas_call | solution.py:564
  34.9 2.3 %shard_map.60 = (f32[16,32,128]{2,1,0:T(8,128)}, f32[768,128]{1,0:T(8,128)}) custom-call(f32[17,40,128]{2,1,0:T(8,128)S(1)} %get-tuple-element.6.x_ref, f32[8,128]{1,0:T(8,128)S(1)} %get-tuple-element.7.iso_ref, s32[1,1,8]{2,1,0:T(1,128)} %vis.1), custom_call_target="tpu_custom_call" | custom-call | tf_op jit(solution)/shard_map/pallas_call | solution.py:594

commit v8 on v6

--- a/solution.py
+++ b/solution.py
@@ -121,7 +121,7 @@
 
 
 def solve_kernel(rhs, scr, act, x_out, iso_out,
-           R, S, M, U1, U2, MZ, SZ, MZ2, SZ2, TA, TB, act_s, ar1, ar2,
+           R, S, M, U1, U2, MZ, SZ, MZ2, SZ2, MZ3, SZ3, TA, TB, TC, act_s, ar1, ar2,
                  lsem, ssem, rsem, asem, arsem, token):
     gx = lax.axis_index("gx")
     gy = lax.axis_index("gy")
@@ -296,16 +296,14 @@
     def total_of(acc, terms):
         return tuple(x + y for x, y in zip(acc, terms))
 
-    def own_terms(value, centre, first, tiles):
+    def own_terms(value, centre, keep):
         terms = []
         for prod in (value * centre, value * value, value):
-            t = [prod[8 * k:8 * k + 8] for k in range(tiles)]
-            if first is None:
-                terms.append((t[0] + t[1]) + t[2])
-            elif tiles == 2:
-                terms.append(jnp.where(sub >= first, t[0], t[1]))
-            else:
-                terms.append((jnp.where(sub >= first, t[0], t[4]) + t[1]) + (t[2] + t[3]))
+            t = [prod[8 * k:8 * k + 8] for k in range(len(keep))]
+            t = [x if c is None else jnp.where(c, x, 0.0) for x, c in zip(t, keep)]
+            while len(t) > 1:
+                t = [x + y for x, y in zip(t[::2], t[1::2])] + t[len(t) - len(t) % 2:]
+            terms.append(t[0])
         return terms
 
     def mask_from(dx, base):
@@ -323,12 +321,26 @@
         sum0 = sum0 + ((v[0:8] + v[8:16]) + (v[16:24] + v[24:32]))
     for p in range(6, 18):
         x_stage(MZ, SZ, TA, p, 16, 32)
-    middle = jnp.concatenate([own[0:8], jnp.where(sub >= 4, own[16:24], own[0:8]), own[16:24]], axis=0)
+    def middle1(dx):
+        k = [jnp.broadcast_to(M[dx, pl.ds(j, 1)], (8, 128)) for j in (1, 2)]
+        return jnp.concatenate([k[0], jnp.where(sub >= 4, k[1], k[0]), k[1]], axis=0)
+
+    def middle2(dx):
+        k = [jnp.broadcast_to(M[dx, pl.ds(j, 1)], (8, 128)) for j in (1, 2)]
+        return jnp.concatenate([k[0], jnp.where(sub >= 2, k[1], k[0])], axis=0)
+
+    def side(p, width):
+        return 0 if p < width else 1 if p < width + 16 else 2
+
+    def first_middle(p, m, acc):
+        value, centre = y_stage(TA, p, 20, 24, m, S[p, pl.ds(12, 24)], R, 12)
+        U1[p, pl.ds(8, 24)] = value
+        return total_of(acc, own_terms(value, centre, [None] * 3)) if 4 <= p < 20 else acc
+
     acc = (zero, zero, zero)
+    m = middle1(1)
     for p in range(6, 18):
-        value, centre = y_stage(TA, p, 20, 24, middle, S[p, pl.ds(12, 24)], R, 12)
-        U1[p, pl.ds(8, 24)] = value
-        acc = total_of(acc, own_terms(value, centre, None, 3))
+        acc = first_middle(p, m, acc)
 
     halo = [p for p in range(28) if not HR <= p < HR + 16]
     outer = [p for p in range(24) if not 6 <= p < 18]
@@ -337,6 +349,26 @@
         z_stage(R, 8, MZ, SZ, 16, p, 32)
     for p in outer:
         x_stage(MZ, SZ, TA, p, 16, 32)
+    receive((2, 1), (0,))
+    m = [middle1(dx) for dx in range(3)]
+    for p in outer:
+        acc = first_middle(p, m[side(p, 4)], acc)
+    for p in range(24):
+        z_stage(U1, 8, MZ2, SZ2, 16, p, 24)
+    for p in range(20):
+        x_stage(MZ2, SZ2, TB, p, 16, 24)
+    m = [middle2(dx) for dx in range(3)]
+    acc2 = (zero, zero, zero)
+    for p in range(20):
+        value, centre = y_stage(TB, p, 18, 16, m[side(p, 2)], S[p + 2, pl.ds(14, 16)], U1, 10)
+        U2[p, pl.ds(8, 16)] = value
+        if 2 <= p < 18:
+            acc2 = total_of(acc2, own_terms(value, centre, [None] * 2))
+    for p in range(20):
+        z_stage(U2, 8, MZ3, SZ3, 16, p, 16)
+    for p in range(16):
+        x_stage(MZ3, SZ3, TC, p, 16, 16)
+
     receive((0,), (1,))
     for p in range(HR, HR + 16):
         z_stage(R, 0, MZ, SZ, 8, p, 8)
@@ -351,42 +383,40 @@
     for p in outer:
         x_stage(MZ, SZ, TA, p, 8, 8)
         x_stage(MZ, SZ, TA, p, 48, 8)
-    receive((2, 1))
+    receive((2, 1), (1, 2))
     masks = [mask_from(dx, -4) for dx in range(3)]
     for p in range(24):
-        dx = 0 if p < 4 else 1 if p < 20 else 2
-        if 6 <= p < 18:
-            low, c_low = y_stage(TA, p, 12, 8, masks[1][0:8], S[p, pl.ds(4, 8)], R, 4)
-            high, c_high = y_stage(TA, p, 44, 8, masks[1][32:40], S[p, pl.ds(36, 8)], R, 36)
-            U1[p, pl.ds(0, 8)] = low
-            U1[p, pl.ds(32, 8)] = high
-            acc = total_of(acc, own_terms(jnp.concatenate([low, high], axis=0),
-                                          jnp.concatenate([c_low, c_high], axis=0), 4, 2))
-        else:
-            value, centre = y_stage(TA, p, 12, 40, masks[dx], S[p, pl.ds(4, 40)], R, 4)
-            U1[p, pl.ds(0, 40)] = value
-            if dx == 1:
-                acc = total_of(acc, own_terms(value, centre, 4, 5))
+        m = masks[side(p, 4)]
+        for row, first, keep in ((0, 4, sub >= 4), (32, 36, sub < 4)):
+            value, centre = y_stage(TA, p, row + 12, 8, m[row:row + 8], S[p, pl.ds(first, 8)], R, first)
+            U1[p, pl.ds(row, 8)] = value
+            if 4 <= p < 20:
+                acc = total_of(acc, own_terms(value, centre, [keep]))
     mu1, mu2, sum1 = acc
 
-    for p in range(0, 24):
-        z_stage(U1, 0, MZ2, SZ2, 8, p, 40)
+    for p in range(24):
+        z_stage(U1, 0, MZ2, SZ2, 8, p, 8)
+        z_stage(U1, 32, MZ2, SZ2, 40, p, 8)
     for p in range(20):
-        x_stage(MZ2, SZ2, TB, p, 8, 40)
+        x_stage(MZ2, SZ2, TB, p, 8, 8)
+        x_stage(MZ2, SZ2, TB, p, 40, 8)
     masks = [mask_from(dx, -2) for dx in range(3)]
-    acc = (zero, zero, zero)
     for p in range(20):
-        dx = 0 if p < 2 else 1 if p < 18 else 2
-        value, centre = y_stage(TB, p, 10, 40, masks[dx], S[p + 2, pl.ds(6, 40)], U1, 2)
-        U2[p, pl.ds(0, 40)] = value
-        if dx == 1:
-            acc = total_of(acc, own_terms(value, centre, 2, 5))
-    mu3, mu4, sum2 = acc
-
-    for p in range(0, 20):
-        z_stage(U2, 0, MZ, SZ, 8, p, 40)
+        m = masks[side(p, 2)]
+        for row, rows, keep in ((0, 8, [sub >= 2]), (24, 16, [None, sub < 2])):
+            value, centre = y_stage(TB, p, row + 10, rows, m[row:row + rows],
+                                    S[p + 2, pl.ds(row + 6, rows)], U1, row + 2)
+            U2[p, pl.ds(row, rows)] = value
+            if 2 <= p < 18:
+                acc2 = total_of(acc2, own_terms(value, centre, keep))
+    mu3, mu4, sum2 = acc2
+
+    for p in range(20):
+        z_stage(U2, 0, MZ3, SZ3, 8, p, 8)
+        z_stage(U2, 24, MZ3, SZ3, 32, p, 16)
     for p in range(16):
-        x_stage(MZ, SZ, TA, p, 8, 40)
+        x_stage(MZ3, SZ3, TC, p, 8, 8)
+        x_stage(MZ3, SZ3, TC, p, 32, 16)
     sub16 = lax.broadcasted_iota(jnp.int32, (16, 128), 0)
     lane16 = lax.broadcasted_iota(jnp.int32, (16, 128), 1)
     lane1 = lax.broadcasted_iota(jnp.int32, (1, 128), 1)
@@ -401,7 +431,7 @@
         coarse = jnp.where(lane1 == k, 1.5 * 2.0 ** (26 + k), coarse)
     mu5 = zero
     for p in range(16):
-        value, centre = y_stage(TA, p, 10, 32, own, S[p + 4, pl.ds(8, 32)], U2, 2)
+        value, centre = y_stage(TC, p, 10, 32, own, S[p + 4, pl.ds(8, 32)], U2, 2)
         w = value * centre
         mu5 = mu5 + ((w[0:8] + w[8:16]) + (w[16:24] + w[24:32]))
 
@@ -426,6 +456,11 @@
     wait = pltpu.make_async_remote_copy(
         ar1.at[pl.ds(0, 31)], ar1.at[pl.ds(0, 31)], asem.at[0], arsem.at[0],
         device_id=(2 * z + 1 - core, gy), device_id_type=MESH)
+    for i, ok in enumerate(has):
+        @pl.when(ok)
+        def _():
+            for c in pieces(i, (0, 1, 2)):
+                c.wait_send()
     wait.wait_recv()
     pending.append(wait)
 
@@ -435,6 +470,7 @@
         pltpu.make_async_remote_copy(
             ar2.at[z], ar2.at[z], asem.at[1], arsem.at[1],
             device_id=(at_z(off), gy), device_id_type=MESH).start()
+    pending.pop().wait_send()
     wait = pltpu.make_async_remote_copy(
         ar2.at[pl.ds(0, 15)], ar2.at[pl.ds(0, 15)], asem.at[1], arsem.at[1],
         device_id=(at_z(1), gy), device_id_type=MESH)
@@ -461,11 +497,6 @@
 
     lax.fori_loop(0, 17, solve, 0, unroll=True)
 
-    for i, ok in enumerate(has):
-        @pl.when(ok)
-        def _():
-            for c in pieces(i, (0, 1, 2)):
-                c.wait_send()
     for c in pending:
         c.wait_send()
 
@@ -553,8 +584,11 @@
             pltpu.VMEM((28, 64, 128), f32),
             pltpu.VMEM((24, 56, 128), f32),
             pltpu.VMEM((24, 56, 128), f32),
+            pltpu.VMEM((20, 56, 128), f32),
+            pltpu.VMEM((20, 56, 128), f32),
             pltpu.VMEM((3, 24, 64, 128), f32),
             pltpu.VMEM((3, 20, 56, 128), f32),
+            pltpu.VMEM((3, 16, 56, 128), f32),
             pltpu.SMEM((1, ACT), jnp.int32),
             pltpu.VMEM((32, 1, 128), f32),
             pltpu.VMEM((16, 1, 128), f32),

time: 37.5 us -> 36.9 us (0.984)
  Pallas kernels: 36.7 us -> 36.1 us
    pallas_call x1, Pallas kernels: 34.4 us -> 33.8 us  [body(): pl.pallas_call(solve_kernel, out_shape=(jax.ShapeDtypeStruct((17, 40, 128...]
where the time goes in v8:
time: 36.9 us; the launch traced here: 36.8 us
  Pallas kernels  36.1 us (98%)
  between operations  0.64 us (2%)
    pallas_call x1, Pallas kernels, body(): pl.pallas_call(solve_kernel, out_shape=(jax.ShapeDtypeStruct((17, 40, 128...  33.8 us
    pallas_call x1, Pallas kernels, body(): pl.pallas_call(crossing_kernel, out_shape=(jax.ShapeDtypeStruct((16, 32,...  2.31 us

profile of v8, /device:TPU:1, one launch (start us, length us, event | category | flops | bytes accessed | tf_op | source)
XLA Modules:
  0.0 36.8 jit_solution(15163821322882009987)
XLA Ops:
  0.6 33.8 %shard_map.59 = (f32[17,40,128]{2,1,0:T(8,128)S(1)}, f32[8,128]{1,0:T(8,128)S(1)}) custom-call(f32[16,32,128]{2,1,0:T(8,128)} %rhs.1, f32[16,32,128]{2,1,0:T(8,128)} %scr.1, s32[1,1,12]{2,1,0:T(1,128)} %act.1), custom_call_target="tpu_custom_call" | custom-call | tf_op jit(solution)/shard_map/pallas_call | solution.py:572
  34.5 2.3 %shard_map.60 = (f32[16,32,128]{2,1,0:T(8,128)}, f32[768,128]{1,0:T(8,128)}) custom-call(f32[17,40,128]{2,1,0:T(8,128)S(1)} %get-tuple-element.6.x_ref, f32[8,128]{1,0:T(8,128)S(1)} %get-tuple-element.7.iso_ref, s32[1,1,8]{2,1,0:T(1,128)} %vis.1), custom_call_target="tpu_custom_call" | custom-call | tf_op jit(solution)/shard_map/pallas_call | solution.py:605

commit v9 on v8

--- a/solution.py
+++ b/solution.py
@@ -144,16 +144,14 @@
     def tell(x, y):
         pl.semaphore_signal(bar, inc=1, device_id=(x, y), device_id_type=MESH)
 
-    other_chip = lax.rem(gx + 2 * core - 1 + NGX, NGX)
-    for dy in (1, -1):
-        tell(other_chip, lax.rem(gy + dy + NGY, NGY))
-    tell(other_chip, gy)
-    for j in (1, 15, 10, 6, 9, 7, 11, 5, 8, 2, 14, 13, 3, 12, 4):
-        for c in (1 - core, core):
-            tell(2 * z + c, lax.rem(gy + j, NGY))
-    tell(2 * z + 1 - core, gy)
-    for off in (4, -4, 3, -3, 2, -2, 1, -1):
-        tell(at_z(off), gy)
+    def along_x(off):
+        return lax.rem(gx + off + NGX, NGX)
+
+    def along_y(off):
+        return lax.rem(gy + off + NGY, NGY)
+
+    for dx, dy in NEIGHBOURS:
+        tell(along_x(dx), along_y(dy))
     has = []
     for dx, dy in NEIGHBOURS:
         ok = None
@@ -214,9 +212,15 @@
 
     lax.fori_loop(0, 16, prepare, 0, unroll=4)
 
-    pl.semaphore_wait(bar, 42)
-    for off in (4, -4):
-        pl.semaphore_signal(token, inc=1, device_id=(at_z(off), gy), device_id_type=MESH)
+    pl.semaphore_wait(bar, 8)
+
+    def vouch(k):
+        for off in (1 << k, -(1 << k)):
+            pl.semaphore_signal(token.at[k], inc=1, device_id=(along_x(off), gy), device_id_type=MESH)
+            if k < 3:
+                pl.semaphore_signal(token.at[k], inc=1, device_id=(gx, along_y(off)), device_id_type=MESH)
+
+    vouch(0)
 
     def pieces(i, which):
         dx, dy = NEIGHBOURS[i]
@@ -350,6 +354,8 @@
     for p in outer:
         x_stage(MZ, SZ, TA, p, 16, 32)
     receive((2, 1), (0,))
+    pl.semaphore_wait(token.at[0], 4)
+    vouch(1)
     m = [middle1(dx) for dx in range(3)]
     for p in outer:
         acc = first_middle(p, m[side(p, 4)], acc)
@@ -369,6 +375,8 @@
     for p in range(16):
         x_stage(MZ3, SZ3, TC, p, 16, 16)
 
+    pl.semaphore_wait(token.at[1], 4)
+    vouch(2)
     receive((0,), (1,))
     for p in range(HR, HR + 16):
         z_stage(R, 0, MZ, SZ, 8, p, 8)
@@ -445,6 +453,7 @@
 
     pending = []
     mine = gy * 2 + core
+    pl.semaphore_wait(token.at[2], 4)
     ar1[mine] = row
     for j in (10, 6, 9, 7, 11, 5, 8, 2, 14, 13, 3, 1, 15, 12, 4, 0):
         for c in (1 - core, core):
@@ -456,6 +465,7 @@
     wait = pltpu.make_async_remote_copy(
         ar1.at[pl.ds(0, 31)], ar1.at[pl.ds(0, 31)], asem.at[0], arsem.at[0],
         device_id=(2 * z + 1 - core, gy), device_id_type=MESH)
+    vouch(3)
     for i, ok in enumerate(has):
         @pl.when(ok)
         def _():
@@ -465,7 +475,7 @@
     pending.append(wait)
 
     ar2[z] = tree([ar1[j] for j in range(32)])
-    pl.semaphore_wait(token, 2)
+    pl.semaphore_wait(token.at[3], 2)
     for off in (8, 7, -7, 6, -6, 5, -5, 4, -4, 3, -3, 2, -2, 1, -1):
         pltpu.make_async_remote_copy(
             ar2.at[z], ar2.at[z], asem.at[1], arsem.at[1],
@@ -597,7 +607,7 @@
             pltpu.SemaphoreType.DMA((8, 3)),
             pltpu.SemaphoreType.DMA((2,)),
             pltpu.SemaphoreType.DMA((2,)),
-            pltpu.SemaphoreType.REGULAR,
+            pltpu.SemaphoreType.REGULAR((4,)),
         ],
         compiler_params=pltpu.CompilerParams(
             collective_id=0, has_side_effects=True, vmem_limit_bytes=32 << 20),

time: 36.9 us -> 39.5 us (1.070)
  Pallas kernels: 36.1 us -> 38.7 us
    pallas_call x1, Pallas kernels: 33.8 us -> 36.4 us  [body(): pl.pallas_call(solve_kernel, out_shape=(jax.ShapeDtypeStruct((17, 40, 128...]
where the time goes in v9:
time: 39.5 us; the launch traced here: 39.4 us
  Pallas kernels  38.7 us (98%)
  between operations  0.64 us (2%)
    pallas_call x1, Pallas kernels, body(): pl.pallas_call(solve_kernel, out_shape=(jax.ShapeDtypeStruct((17, 40, 128...  36.4 us
    pallas_call x1, Pallas kernels, body(): pl.pallas_call(crossing_kernel, out_shape=(jax.ShapeDtypeStruct((16, 32,...  2.31 us

profile of v9, /device:TPU:1, one launch (start us, length us, event | category | flops | bytes accessed | tf_op | source)
XLA Modules:
  0.0 39.4 jit_solution(16949676479633934836)
XLA Ops:
  0.6 36.4 %shard_map.59 = (f32[17,40,128]{2,1,0:T(8,128)S(1)}, f32[8,128]{1,0:T(8,128)S(1)}) custom-call(f32[16,32,128]{2,1,0:T(8,128)} %rhs.1, f32[16,32,128]{2,1,0:T(8,128)} %scr.1, s32[1,1,12]{2,1,0:T(1,128)} %act.1), custom_call_target="tpu_custom_call" | custom-call | tf_op jit(solution)/shard_map/pallas_call | solution.py:582
  37.1 2.3 %shard_map.60 = (f32[16,32,128]{2,1,0:T(8,128)}, f32[768,128]{1,0:T(8,128)}) custom-call(f32[17,40,128]{2,1,0:T(8,128)S(1)} %get-tuple-element.6.x_ref, f32[8,128]{1,0:T(8,128)S(1)} %get-tuple-element.7.iso_ref, s32[1,1,8]{2,1,0:T(1,128)} %vis.1), custom_call_target="tpu_custom_call" | custom-call | tf_op jit(solution)/shard_map/pallas_call | solution.py:615

commit v10 on v8

--- a/solution.py
+++ b/solution.py
@@ -250,9 +250,9 @@
                 for c in pieces(i, which):
                     c.wait_recv()
 
-    for which in ((0,), (2, 1)):
-        for i, ok in enumerate(has):
-            @pl.when(ok)
+    for which, order in (((0,), range(8)), ((2, 1), (6, 7, 4, 5, 0, 1, 2, 3))):
+        for i in order:
+            @pl.when(has[i])
             def _():
                 for c in pieces(i, which):
                     c.start()
@@ -518,11 +518,6 @@
     empty = sigmoid4(0.0 - iso[0:32])
     group = lane // BLK
     odd = [(group // (1 << bit)) % 2 == 1 for bit in range(3)]
-    load.wait()
-    slots = []
-    for q in range(VIS):
-        n = vis_s[0, q]
-        slots.append(jnp.where(n >= 0, n, 16) * 96)
     stores = [store]
     for e in range(3):
         for p in range(16):
@@ -553,6 +548,12 @@
                 w, ib = part % 2, part // 2
                 for t in range(8):
                     BR[pl.ds((w * 8 + t) * 96 + e * 32 + ib * 8, 8)] = vs[part][t]
+        if e == 0:
+            load.wait()
+            slots = []
+            for q in range(VIS):
+                n = vis_s[0, q]
+                slots.append(jnp.where(n >= 0, n, 16) * 96)
         for q in range(VIS):
             start = pl.multiple_of(slots[q] + e * 32, 8)
             stores.append(pltpu.make_async_copy(

time: 36.9 us -> 37.3 us (1.011)
  Pallas kernels: 36.1 us -> 36.5 us
    pallas_call x1, Pallas kernels: 33.8 us -> 34.4 us  [body(): pl.pallas_call(solve_kernel, out_shape=(jax.ShapeDtypeStruct((17, 40, 128...]
where the time goes in v10:
time: 37.3 us; the launch traced here: 37.2 us
  Pallas kernels  36.5 us (98%)
  between operations  0.64 us (2%)
    pallas_call x1, Pallas kernels, body(): pl.pallas_call(solve_kernel, out_shape=(jax.ShapeDtypeStruct((17, 40, 128...  34.4 us
    pallas_call x1, Pallas kernels, body(): pl.pallas_call(crossing_kernel, out_shape=(jax.ShapeDtypeStruct((16, 32,...  2.11 us

profile of v10, /device:TPU:1, one launch (start us, length us, event | category | flops | bytes accessed | tf_op | source)
XLA Modules:
  0.0 37.2 jit_solution(7947206721145469816)
XLA Ops:
  0.6 34.4 %shard_map.59 = (f32[17,40,128]{2,1,0:T(8,128)S(1)}, f32[8,128]{1,0:T(8,128)S(1)}) custom-call(f32[16,32,128]{2,1,0:T(8,128)} %rhs.1, f32[16,32,128]{2,1,0:T(8,128)} %scr.1, s32[1,1,12]{2,1,0:T(1,128)} %act.1), custom_call_target="tpu_custom_call" | custom-call | tf_op jit(solution)/shard_map/pallas_call | solution.py:573
  35.1 2.1 %shard_map.60 = (f32[16,32,128]{2,1,0:T(8,128)}, f32[768,128]{1,0:T(8,128)}) custom-call(f32[17,40,128]{2,1,0:T(8,128)S(1)} %get-tuple-element.6.x_ref, f32[8,128]{1,0:T(8,128)S(1)} %get-tuple-element.7.iso_ref, s32[1,1,8]{2,1,0:T(1,128)} %vis.1), custom_call_target="tpu_custom_call" | custom-call | tf_op jit(solution)/shard_map/pallas_call | solution.py:606

commit v11 on v10

--- a/solution.py
+++ b/solution.py
@@ -250,9 +250,9 @@
                 for c in pieces(i, which):
                     c.wait_recv()
 
-    for which, order in (((0,), range(8)), ((2, 1), (6, 7, 4, 5, 0, 1, 2, 3))):
-        for i in order:
-            @pl.when(has[i])
+    for which in ((0,), (2, 1)):
+        for i, ok in enumerate(has):
+            @pl.when(ok)
             def _():
                 for c in pieces(i, which):
                     c.start()

time: 37.3 us -> 36.7 us (0.984)
  Pallas kernels: 36.5 us -> 35.9 us
    pallas_call x1, Pallas kernels: 34.4 us -> 33.8 us  [body(): pl.pallas_call(solve_kernel, out_shape=(jax.ShapeDtypeStruct((17, 40, 128...]
where the time goes in v11:
time: 36.7 us; the launch traced here: 36.6 us
  Pallas kernels  35.9 us (98%)
  between operations  0.64 us (2%)
    pallas_call x1, Pallas kernels, body(): pl.pallas_call(solve_kernel, out_shape=(jax.ShapeDtypeStruct((17, 40, 128...  33.8 us
    pallas_call x1, Pallas kernels, body(): pl.pallas_call(crossing_kernel, out_shape=(jax.ShapeDtypeStruct((16, 32,...  2.11 us

profile of v11, /device:TPU:1, one launch (start us, length us, event | category | flops | bytes accessed | tf_op | source)
XLA Modules:
  0.0 36.6 jit_solution(10389439927025652586)
XLA Ops:
  0.6 33.8 %shard_map.59 = (f32[17,40,128]{2,1,0:T(8,128)S(1)}, f32[8,128]{1,0:T(8,128)S(1)}) custom-call(f32[16,32,128]{2,1,0:T(8,128)} %rhs.1, f32[16,32,128]{2,1,0:T(8,128)} %scr.1, s32[1,1,12]{2,1,0:T(1,128)} %act.1), custom_call_target="tpu_custom_call" | custom-call | tf_op jit(solution)/shard_map/pallas_call | solution.py:573
  34.5 2.1 %shard_map.60 = (f32[16,32,128]{2,1,0:T(8,128)}, f32[768,128]{1,0:T(8,128)}) custom-call(f32[17,40,128]{2,1,0:T(8,128)S(1)} %get-tuple-element.6.x_ref, f32[8,128]{1,0:T(8,128)S(1)} %get-tuple-element.7.iso_ref, s32[1,1,8]{2,1,0:T(1,128)} %vis.1), custom_call_target="tpu_custom_call" | custom-call | tf_op jit(solution)/shard_map/pallas_call | solution.py:606

commit v12 on v10

--- a/solution.py
+++ b/solution.py
@@ -250,7 +250,7 @@
                 for c in pieces(i, which):
                     c.wait_recv()
 
-    for which, order in (((0,), range(8)), ((2, 1), (6, 7, 4, 5, 0, 1, 2, 3))):
+    for which, order in (((0,), (6, 7, 0, 1, 2, 3, 4, 5)), ((2, 1), range(8))):
         for i in order:
             @pl.when(has[i])
             def _():

time: 37.3 us -> 36.7 us (0.984)
  Pallas kernels: 36.5 us -> 36 us
    pallas_call x1, Pallas kernels: 34.4 us -> 33.9 us  [body(): pl.pallas_call(solve_kernel, out_shape=(jax.ShapeDtypeStruct((17, 40, 128...]
where the time goes in v12:
time: 36.7 us; the launch traced here: 36.6 us
  Pallas kernels  36 us (98%)
  between operations  0.64 us (2%)
    pallas_call x1, Pallas kernels, body(): pl.pallas_call(solve_kernel, out_shape=(jax.ShapeDtypeStruct((17, 40, 128...  33.9 us
    pallas_call x1, Pallas kernels, body(): pl.pallas_call(crossing_kernel, out_shape=(jax.ShapeDtypeStruct((16, 32,...  2.11 us

profile of v12, /device:TPU:1, one launch (start us, length us, event | category | flops | bytes accessed | tf_op | source)
XLA Modules:
  0.0 36.6 jit_solution(2728488048355247628)
XLA Ops:
  0.6 33.9 %shard_map.59 = (f32[17,40,128]{2,1,0:T(8,128)S(1)}, f32[8,128]{1,0:T(8,128)S(1)}) custom-call(f32[16,32,128]{2,1,0:T(8,128)} %rhs.1, f32[16,32,128]{2,1,0:T(8,128)} %scr.1, s32[1,1,12]{2,1,0:T(1,128)} %act.1), custom_call_target="tpu_custom_call" | custom-call | tf_op jit(solution)/shard_map/pallas_call | solution.py:573
  34.5 2.1 %shard_map.60 = (f32[16,32,128]{2,1,0:T(8,128)}, f32[768,128]{1,0:T(8,128)}) custom-call(f32[17,40,128]{2,1,0:T(8,128)S(1)} %get-tuple-element.6.x_ref, f32[8,128]{1,0:T(8,128)S(1)} %get-tuple-element.7.iso_ref, s32[1,1,8]{2,1,0:T(1,128)} %vis.1), custom_call_target="tpu_custom_call" | custom-call | tf_op jit(solution)/shard_map/pallas_call | solution.py:606
